TPU v7x, 32 devices: a whole 2x2x4 slice. The times are simulated.
32 devices in a mesh: ctx: 16 (over z, y, core), head: 2 (over x).
Axes of the slice: x: 2, y: 2, z: 4, core: 2. Of those that a mesh axis runs over, the one named last changes fastest.
Arguments:
- queries: bfloat16 [8192, 2048], P('ctx', 'head'), may hold values from -6 to 6
- keys: bfloat16 [8192, 2048], P('ctx', 'head'), may hold values from -6 to 6
- values: bfloat16 [8192, 2048], P('ctx', 'head'), may hold values from -6 to 6
- rates: float32 [8192, 2], P('ctx', 'head'), may hold values from 0.0005524272 to 0.0055242716
- w_up: bfloat16 [2, 1024, 512], P('head'), may hold values from -0.1875 to 0.1875
- w_gate: bfloat16 [2, 1024, 512], P('head'), may hold values from -0.1875 to 0.1875
- w_down: bfloat16 [2, 512, 1024], P('head'), may hold values from -0.25 to 0.25
- w_out: bfloat16 [2048, 5120], P('head'), may hold values from -0.125 to 0.125
Outputs:
- mixed: bfloat16 [8192, 5120], P('ctx', 'head')
All inputs are finite; a program needn't handle non-finite values.
Results may differ from a plain program's by a relative error of at most 0.018.
Values may be sent and summed in bfloat16 or wider, within the bound.
A program may use at most 128 MiB of HBM per device.

v0:
```python
import functools

import jax
import jax.numpy as jnp
from jax import lax
from jax.experimental import pallas as pl
from jax.experimental.pallas import tpu as pltpu
from jax.sharding import PartitionSpec as P

STEPS = 2
F32 = jnp.float32
BF16 = jnp.bfloat16
MESH = pl.DeviceIdType.MESH
GROUP = 3


PARTS = 4


def orders_of(n_ctx):
    count = n_ctx.bit_length() - 1
    middle, low, high = list(range(1, count - 2)), count - 2, count - 1
    return [
        [0] + middle + [low, high],
        [0] + middle + [high, low],
        [0, low, high] + middle,
        [0, high, low] + middle,
    ]


def raw_bit(me, bit):
    return (me // (1 << bit)) % 2


def half_of(me, stage, count):
    if stage == count - 2:
        return (raw_bit(me, count - 2) + raw_bit(me, count - 1)) % 2
    return raw_bit(me, stage)


def partner_of(me, stage, count):
    flips = (count - 2, count - 1) if stage == count - 1 else (stage,)
    for bit in flips:
        me = me + (1 - 2 * raw_bit(me, bit)) * (1 << bit)
    return me


def lanes_of(part, cols):
    width = cols // PARTS
    return slice(part * width, (part + 1) * width)


def dot(left, right, dims=((1,), (0,))):
    return lax.dot_general(left, right, (dims, ((), ())), preferred_element_type=F32)


def square_sum(block):
    return jnp.sum((block * block).reshape(-1, 8, block.shape[-1]), axis=0)


def layer_kernel(
    n_ctx, q, k, v, r, w0, w1, w2, w_out, out, *scratch
):
    count = n_ctx.bit_length() - 1
    recvs, scratch = scratch[:count], scratch[count:]
    accs, scratch = scratch[: count - 1], scratch[count - 1 :]
    (
        kt, u, ut, first2, grads, blocks, mid, kept, sums,
        w_near, w_far, near, far, total_out,
        send_sem, recv_sem, swap_send, swap_recv, share_sem, local_sem,
    ) = scratch
    tokens, rows = k.shape
    cols = w0.shape[1]
    half = w_out.shape[1] // 2
    orders = orders_of(n_ctx)
    me = lax.axis_index("ctx")
    head = lax.axis_index("head")

    def bit_of(stage):
        return half_of(me, stage, count)

    def partner(stage):
        return {"ctx": partner_of(me, stage, count)}

    def start_of(order):
        start, left = 0, rows
        for stage in order:
            left = left // 2
            start = start + bit_of(stage) * left
        return start

    across = {"head": 1 - head}
    barrier = pltpu.get_barrier_semaphore()
    for target in [partner(stage) for stage in range(count)] + [across]:
        pl.semaphore_signal(barrier, inc=1, device_id=target, device_id_type=MESH)
    pl.semaphore_wait(barrier, count + 1)

    def swap(slot, source, target):
        return pltpu.make_async_remote_copy(
            src_ref=source,
            dst_ref=target,
            send_sem=swap_send.at[slot],
            recv_sem=swap_recv.at[slot],
            device_id=across,
            device_id_type=MESH,
        )

    near_cols = pl.ds(pl.multiple_of(head * half, 128), half)
    far_cols = pl.ds(pl.multiple_of((1 - head) * half, 128), half)
    depth = rows // 2
    own_rows = pl.ds(pl.multiple_of(raw_bit(me, 0) * depth, depth), depth)
    w_swap = swap(0, w_out.at[own_rows, far_cols], w_far.at[own_rows, :])
    w_swap.start()
    w_copy = pltpu.make_async_copy(w_out.at[:, near_cols], w_near, local_sem)
    w_copy.start()

    tile = tokens // 4
    for t in range(4):
        at = slice(t * tile, (t + 1) * tile)
        scaled = (r[at, :] * v[at, :].astype(F32)).astype(BF16)
        u[at, :] = scaled
        ut[:, at] = scaled.T
        kt[:, at] = k[at, :].T
    for t in range(cols // 128):
        at = slice(t * 128, (t + 1) * 128)
        first2[:, at] = w2[at, :].T

    chains = [(w, part) for w in range(GROUP) for part in range(PARTS)]
    firsts = (w0, w1, first2)
    scales = [None] * GROUP
    for step in range(STEPS):
        now = firsts if step == 0 else [blocks.at[w] for w in range(GROUP)]
        copies = {}

        def scaled_dot(w, left):
            product = dot(left, now[w][...])
            return product if scales[w] is None else product * scales[w]

        for t in range(2):
            at = slice(t * (tokens // 2), (t + 1) * (tokens // 2))
            act = scaled_dot(0, k[at, :])
            lin = scaled_dot(1, k[at, :])
            err = scaled_dot(2, u[at, :])
            sig = jax.nn.sigmoid(act)
            gate = act * sig
            mid[0, at, :] = (err * lin * sig * (1.0 + act * (1.0 - sig))).astype(BF16)
            mid[1, at, :] = (err * gate).astype(BF16)
            mid[2, at, :] = (gate * lin).astype(BF16)

        def send(chain, slot, source, target, bit):
            copy = pltpu.make_async_remote_copy(
                src_ref=source,
                dst_ref=target,
                send_sem=send_sem.at[chain, slot],
                recv_sem=recv_sem.at[chain, slot],
                device_id=partner(bit),
                device_id_type=MESH,
            )
            copy.start()
            copies[chain, slot] = copy

        def send_down(chain, stage):
            w, part = chains[chain]
            lanes = lanes_of(part, cols)
            bit = orders[part][stage]
            size = rows >> (stage + 1)
            away = pl.ds(pl.multiple_of((1 - bit_of(bit)) * size, size), size)
            origin = grads if stage == 0 else accs[stage - 1]
            source = origin.at[w, away, lanes]
            send(chain, stage, source, recvs[stage].at[w, :, lanes], bit)

        def region(chain, stage):
            w, part = chains[chain]
            size = rows >> stage
            start = start_of(orders[part][:stage])
            return pl.ds(pl.multiple_of(start, size), size)

        def send_up(chain, stage):
            w, part = chains[chain]
            place = blocks.at[w, region(chain, stage + 1), lanes_of(part, cols)]
            send(chain, 2 * count - 1 - stage, place, place, orders[part][stage])

        for w in range(GROUP):
            left = ut if w == 2 else kt

            def grad_rows(piece, carry):
                at = pl.ds(pl.multiple_of(piece * (rows // 4), rows // 4), rows // 4)
                grads[w, at, :] = dot(left[at, :], mid[w]).astype(BF16)
                return carry

            lax.fori_loop(0, 4, grad_rows, 0)
            for part in range(PARTS):
                send_down(PARTS * w + part, 0)
        if step == 0:
            norms = [
                jnp.sqrt(jnp.sum(square_sum(b[...].astype(F32)), keepdims=True))
                for b in firsts
            ]
        for stage in range(count):
            size = rows >> (stage + 1)
            for chain, (w, part) in enumerate(chains):
                lanes = lanes_of(part, cols)
                bit = orders[part][stage]
                close = pl.ds(pl.multiple_of(bit_of(bit) * size, size), size)
                copies[chain, stage].wait_recv()
                origin = grads if stage == 0 else accs[stage - 1]
                held = origin[w, close, lanes].astype(F32)
                total = held + recvs[stage][w, :, lanes].astype(F32)
                if stage < count - 1:
                    accs[stage][w, :, lanes] = total.astype(BF16)
                    send_down(chain, stage + 1)
                else:
                    place = region(chain, count)
                    if step == 0:
                        moved = firsts[w][place, lanes].astype(F32) + total
                    else:
                        moved = kept[w, :, lanes] * scales[w] + total
                    kept[w, :, lanes] = moved
                    rounded = moved.astype(BF16)
                    blocks[w, place, lanes] = rounded
                    send_up(chain, count - 1)
                    sums[w, :, lanes] = square_sum(rounded.astype(F32))
        for stage in reversed(range(count)):
            size = rows >> (stage + 1)
            for chain, (w, part) in enumerate(chains):
                lanes = lanes_of(part, cols)
                copies[chain, 2 * count - 1 - stage].wait_recv()
                if stage > 0:
                    send_up(chain, stage - 1)
                other = start_of(orders[part][:stage])
                other = other + (1 - bit_of(orders[part][stage])) * size
                place = pl.ds(pl.multiple_of(other, size), size)
                sums[w, :, lanes] += square_sum(blocks[w, place, lanes].astype(F32))
        for copy in copies.values():
            copy.wait_send()
        scales = [
            norms[w] / jnp.sqrt(jnp.sum(sums[w], keepdims=True) + 1e-06)
            for w in range(GROUP)
        ]

    w_swap.wait()
    w_share = pltpu.make_async_remote_copy(
        src_ref=w_far.at[own_rows, :],
        dst_ref=w_far.at[own_rows, :],
        send_sem=share_sem.at[0],
        recv_sem=share_sem.at[1],
        device_id=partner(0),
        device_id_type=MESH,
    )
    w_share.start()
    o_swaps = []
    for t in range(4):
        at = slice(t * tile, (t + 1) * tile)
        act = dot(q[at, :], blocks[0]) * scales[0]
        lin = dot(q[at, :], blocks[1]) * scales[1]
        hidq = (act * jax.nn.sigmoid(act) * lin).astype(BF16)
        piece = dot(hidq, blocks[2], ((1,), (1,))) * scales[2]
        near[at, :] = piece.astype(BF16)
        o_swap = swap(1 + t, near.at[at, :], far.at[at, :])
        o_swap.start()
        o_swaps.append(o_swap)
    w_copy.wait()
    width = half // 5

    def near_cols_of(c, carry):
        lanes = pl.ds(pl.multiple_of(c * width, 128), width)
        total_out[:, lanes] = dot(near[...], w_near[:, lanes])
        return carry

    lax.fori_loop(0, 5, near_cols_of, 0)
    w_share.wait()
    for t in range(4):
        at = slice(t * tile, (t + 1) * tile)
        o_swaps[t].wait_recv()

        def far_cols_of(c, carry):
            lanes = pl.ds(pl.multiple_of(c * width, 128), width)
            added = total_out[at, lanes] + dot(far[at, :], w_far[:, lanes])
            out[at, lanes] = added.astype(BF16)
            return carry

        lax.fori_loop(0, 5, far_cols_of, 0)
    for o_swap in o_swaps:
        o_swap.wait_send()


def shards(n_ctx, queries, keys, values, rates, w_up, w_gate, w_down, w_out):
    tokens, rows = keys.shape
    cols = w_up.shape[2]
    half = w_out.shape[1] // 2
    count = n_ctx.bit_length() - 1
    chains = PARTS * GROUP
    vmem = pl.BlockSpec(memory_space=pltpu.VMEM)
    return pl.pallas_call(
        functools.partial(layer_kernel, n_ctx),
        out_shape=jax.ShapeDtypeStruct((tokens, half), BF16),
        in_specs=[vmem] * 7 + [pl.BlockSpec(memory_space=pl.ANY)],
        out_specs=vmem,
        scratch_shapes=[
            pltpu.VMEM((GROUP, rows >> (stage + 1), cols), BF16)
            for stage in range(count)
        ]
        + [
            pltpu.VMEM((GROUP, rows >> (stage + 1), cols), BF16)
            for stage in range(count - 1)
        ]
        + [
            pltpu.VMEM((rows, tokens), BF16),
            pltpu.VMEM((tokens, rows), BF16),
            pltpu.VMEM((rows, tokens), BF16),
            pltpu.VMEM((rows, cols), BF16),
            pltpu.VMEM((GROUP, rows, cols), BF16),
            pltpu.VMEM((GROUP, rows, cols), BF16),
            pltpu.VMEM((GROUP, tokens, cols), BF16),
            pltpu.VMEM((GROUP, rows // n_ctx, cols), F32),
            pltpu.VMEM((GROUP, 8, cols), F32),
            pltpu.VMEM((rows, half), BF16),
            pltpu.VMEM((rows, half), BF16),
            pltpu.VMEM((tokens, rows), BF16),
            pltpu.VMEM((tokens, rows), BF16),
            pltpu.VMEM((tokens, half), F32),
            pltpu.SemaphoreType.DMA((chains, 2 * count)),
            pltpu.SemaphoreType.DMA((chains, 2 * count)),
            pltpu.SemaphoreType.DMA((5,)),
            pltpu.SemaphoreType.DMA((5,)),
            pltpu.SemaphoreType.DMA((2,)),
            pltpu.SemaphoreType.DMA,
        ],
        compiler_params=pltpu.CompilerParams(
            collective_id=0, has_side_effects=True, vmem_limit_bytes=60 << 20
        ),
    )(queries, keys, values, rates, w_up[0], w_gate[0], w_down[0], w_out)


def solution(mesh):
    def body(*args):
        return shards(mesh.shape["ctx"], *args)

    return jax.shard_map(
        body,
        mesh=mesh,
        in_specs=(
            P("ctx", "head"),
            P("ctx", "head"),
            P("ctx", "head"),
            P("ctx", "head"),
            P("head", None, None),
            P("head", None, None),
            P("head", None, None),
            P("head", None),
        ),
        out_specs=P("ctx", "head"),
        check_vma=False,
    )
```

profile of v0, /device:TPU:0, one launch (start us, length us, event | category | flops | bytes accessed | tf_op | source)
XLA Modules:
  0.0 143.2 jit_solution(14941814637520161725)
XLA Ops:
  0.0 1.5 %copy.9.r = f32[512,1]{1,0:T(8,128)} copy(f32[512,1]{0,1:T(1,128)} %param.11) | data formatting | bytes 4096 | tf_op args[3]
  1.5 138.2 %shard_map.82 = bf16[512,2560]{1,0:T(8,128)(2,1)} custom-call(bf16[512,1024]{1,0:T(8,128)(2,1)} %q.1, bf16[512,1024]{1,0:T(8,128)(2,1)} %k.1, bf16[512,1024]{1,0:T(8,128)(2,1)} %v.1, f32[512,1]{1,0:T(8,128)} %copy.9.r, bf16[1024,512]{1,0:T(8,128)(2,1)} %bitcast.3, bf16[1024,512]{1,0:T(8,128)(2,1)} %bitcast.4, bf16[512,1024]{1,0:T(8,128)(2,1)} %bitcast.5, ...), custom_call_target="tpu_custom_call" | custom-call | tf_op jit(solution)/shard_map/pallas_call | solution.py:294
  139.8 3.4 %copy.11 = bf16[512,2560]{1,0:T(8,128)(2,1)} copy(bf16[512,2560]{1,0:T(8,128)(2,1)} %shard_map.82) | data formatting | bytes 5242880
where the time goes:
time: 143 us
  Pallas kernels  138 us (97%)
  local copies, waits for them, and re-layouts  4.93 us (3%)
    pallas_call x1, Pallas kernels, shards(): pl.pallas_call(functools.partial(layer_kernel, n_ctx), out_shape=jax.Shap...  138 us
    unnamed x2, local copies, waits for them, and re-layouts  4.93 us

commit v1 on v0

v1 whole, which is shorter than its diff:
```python
import functools

import jax
import jax.numpy as jnp
from jax import lax
from jax.experimental import pallas as pl
from jax.experimental.pallas import tpu as pltpu
from jax.sharding import PartitionSpec as P

STEPS = 2
F32 = jnp.float32
BF16 = jnp.bfloat16
MESH = pl.DeviceIdType.MESH
GROUP = 3
LANE_PARTS = 2
CORES = 2
RING_ROWS = 4
TILES = 4
ORDERS = ((0, 1, 2), (2, 0, 1))


def ring_place(chip, width):
    row, turn = chip // width, width - 1 - chip % width
    odd = turn % 2
    along = (1 - odd) * (row - 1) + odd * (RING_ROWS - 1 - row)
    return jnp.where(row == 0, chip, width + (RING_ROWS - 1) * turn + along)


def ring_chip(place, width):
    past = jnp.maximum(place - width, 0)
    turn, along = past // (RING_ROWS - 1), past % (RING_ROWS - 1)
    odd = turn % 2
    row = (1 - odd) * (1 + along) + odd * (RING_ROWS - 1 - along)
    return jnp.where(place < width, place, row * width + width - 1 - turn)


def dot(left, right, dims=((1,), (0,))):
    return lax.dot_general(left, right, (dims, ((), ())), preferred_element_type=F32)


def square_sum(block):
    return jnp.sum((block * block).reshape(-1, 8, block.shape[-1]), axis=0)


def lane_fold(block):
    return block[:, :128] + block[:, 128:]


def layer_kernel(n_ctx, q, k, v, r, w0, w1, w2, w_out, out, *scratch):
    (
        ks, us, qs, vin, kt, ut, first0, first1, in2, first2,
        acts, mid, grads, blocks, arrived, kept, tally, tally_in, norm_sums,
        hq, near_hid, far_hid, near_w2, far_w2, far_scale, scale_out,
        w_near, w_far, near, total_out,
        ring_send, ring_recv, pair_send, pair_recv, tally_send, tally_recv,
        side_send, side_recv, w2_send, w2_recv, hid_send, hid_recv, local_sem,
    ) = scratch
    tokens, rows = k.shape
    cols = first0.shape[1]
    half = w_out.shape[1] // 2
    ring = n_ctx // CORES
    width = ring // RING_ROWS
    size = rows // ring
    bits = n_ctx.bit_length() - 1
    me = lax.axis_index("ctx")
    head = lax.axis_index("head")
    core = me % CORES
    chip = me // CORES
    place = ring_place(chip, width)
    right = {"ctx": ring_chip((place + 1) % ring, width) * CORES + core}
    left = {"ctx": ring_chip((place + ring - 1) % ring, width) * CORES + core}
    sibling = {"ctx": chip * CORES + 1 - core}
    across = {"head": 1 - head}
    diagonal = {"ctx": chip * CORES + 1 - core, "head": 1 - head}
    tally_partners = [
        {"ctx": me + (1 - 2 * ((me // (1 << bit)) % 2)) * (1 << bit)}
        for bit in range(bits)
    ]

    def remote(source, target, send_sem, recv_sem, device):
        return pltpu.make_async_remote_copy(
            src_ref=source,
            dst_ref=target,
            send_sem=send_sem,
            recv_sem=recv_sem,
            device_id=device,
            device_id_type=MESH,
        )

    def local(slot, source, target):
        return pltpu.make_async_copy(source, target, local_sem.at[slot])

    own_cols = pl.ds(pl.multiple_of(core * cols, 128), cols)
    own, other = slice(0, tokens), slice(tokens, 2 * tokens)
    loads = [
        local(0, k, ks.at[own, :]),
        local(1, v, vin),
        local(2, w0.at[:, own_cols], first0),
        local(3, w1.at[:, own_cols], first1),
        local(4, w2.at[pl.ds(pl.multiple_of(core * cols, 128), cols), :], in2),
        local(5, q, qs.at[own, :]),
    ]
    for load in loads:
        load.start()

    partners = [right, left, sibling, across, diagonal] + tally_partners
    barrier = pltpu.get_barrier_semaphore()
    for target in partners:
        pl.semaphore_signal(barrier, inc=1, device_id=target, device_id_type=MESH)
    pl.semaphore_wait(barrier, len(partners))

    def pair(slot, source, target):
        return remote(source, target, pair_send.at[slot], pair_recv.at[slot], sibling)

    k_pair = pair(0, k, ks.at[other, :])
    k_pair.start()
    near_cols = pl.ds(pl.multiple_of(head * half, 128), half)
    far_cols = pl.ds(pl.multiple_of((1 - head) * half, 128), half)
    depth = rows // CORES
    own_rows = pl.ds(pl.multiple_of(core * depth, depth), depth)
    w_swap = remote(
        w_out.at[own_rows, far_cols], w_far.at[own_rows, :],
        side_send.at[0], side_recv.at[0], across,
    )
    w_swap.start()

    loads[1].wait()
    rate = jnp.broadcast_to(r[...], (128, tokens)).T
    for t in range(rows // 128):
        at = slice(t * 128, (t + 1) * 128)
        scaled = (rate * vin[:, at].astype(F32)).astype(BF16)
        us[own, at] = scaled
        ut[at, own] = scaled.T
    u_pair = pair(1, us.at[own, :], us.at[other, :])
    u_pair.start()
    loads[0].wait()
    for t in range(rows // 128):
        at = slice(t * 128, (t + 1) * 128)
        kt[at, own] = ks[own, at].T
    kt_pair = pair(2, kt.at[:, own], kt.at[:, other])
    kt_pair.start()
    ut_pair = pair(3, ut.at[:, own], ut.at[:, other])
    ut_pair.start()
    q_pair = pair(4, q, qs.at[other, :])
    q_pair.start()
    w_copy = local(6, w_out.at[:, near_cols], w_near)
    w_copy.start()
    for load in loads[2:5]:
        load.wait()
    for t in range(rows // 128):
        at = slice(t * 128, (t + 1) * 128)
        first2[at, :] = in2[:, at].T

    firsts = (first0, first1, first2)
    scales = [None] * GROUP

    def weight(step, w):
        if step == 0:
            return firsts[w][...]
        return jnp.concatenate([blocks[2 * w], blocks[2 * w + 1]], axis=1)

    def act_dot(step, w, source, at):
        product = dot(source[at, :], weight(step, w))
        acts[w, at, :] = product

    for w, source in enumerate((ks, ks, us)):
        act_dot(0, w, source, own)
    k_pair.wait_recv()
    for w in range(2):
        act_dot(0, w, ks, other)
    u_pair.wait_recv()
    act_dot(0, 2, us, other)

    flows = [(w, h) for w in range(GROUP) for h in range(LANE_PARTS)]

    def reach(h):
        longer = ring // 2
        return (longer, ring - 1 - longer) if h == 0 else (ring - 1 - longer, longer)

    def chunk(number):
        return pl.ds(pl.multiple_of((number % ring) * size, size), size)

    for step in range(STEPS):
        order = ORDERS[step % 2]
        copies = {}

        def gates(piece, carry):
            at = pl.ds(pl.multiple_of(piece * 128, 128), 128)
            act, lin, err = acts[0, at, :], acts[1, at, :], acts[2, at, :]
            if step > 0:
                act, lin, err = act * scales[0], lin * scales[1], err * scales[2]
            sig = jax.nn.sigmoid(act)
            gate = act * sig
            mid[0, at, :] = (err * lin * sig * (1.0 + act * (1.0 - sig))).astype(BF16)
            mid[1, at, :] = (err * gate).astype(BF16)
            mid[2, at, :] = (gate * lin).astype(BF16)
            return carry

        lax.fori_loop(0, 2 * tokens // 128, gates, 0)
        if step == 0:
            kt_pair.wait_recv()
            ut_pair.wait_recv()

        def send(flow, slot, source, target, device):
            copy = remote(
                source, target, ring_send.at[flow, slot], ring_recv.at[flow, slot], device
            )
            copy.start()
            copies[flow, slot] = copy

        def send_sum(flow, to_right, s):
            far, back = reach(flow % LANE_PARTS)
            at = chunk(place + far - s) if to_right else chunk(place + ring - back + s)
            slot = s if to_right else far + s
            device = right if to_right else left
            send(flow, slot, grads.at[flow, at, :], arrived.at[flow, slot], device)

        def send_block(flow, to_right, t):
            far, back = reach(flow % LANE_PARTS)
            at = chunk(place + ring - t) if to_right else chunk(place + t)
            slot = ring - 1 + (t if to_right else far + t)
            device = right if to_right else left
            here = blocks.at[flow, at, :]
            send(flow, slot, here, here, device)

        def pass_sum(flow, to_right, s):
            far, back = reach(flow % LANE_PARTS)
            slot = s if to_right else far + s
            at = chunk(place + far - 1 - s) if to_right else chunk(place + ring + 1 - back + s)
            copies[flow, slot].wait_recv()
            total = grads[flow, at, :].astype(F32) + arrived[flow, slot].astype(F32)
            grads[flow, at, :] = total.astype(BF16)
            send_sum(flow, to_right, s + 1)

        w2_copies = []

        def send_w2(flow, number):
            h = flow % LANE_PARTS
            here = chunk(number)
            slot = len(w2_copies)
            copy = remote(
                blocks.at[flow, here, :], far_w2.at[h, here, :],
                w2_send.at[slot], w2_recv.at[slot], across,
            )
            copy.start()
            w2_copies.append(copy)

        for w in order:
            source = ut if w == 2 else kt

            def grad_rows(piece, carry):
                at = pl.ds(pl.multiple_of(piece * (rows // 4), rows // 4), rows // 4)
                product = dot(source[at, :], mid[w]).astype(BF16)
                grads[2 * w, at, :] = product[:, :128]
                grads[2 * w + 1, at, :] = product[:, 128:]
                return carry

            lax.fori_loop(0, 4, grad_rows, 0)
            for h in range(LANE_PARTS):
                send_sum(2 * w + h, True, 0)
                send_sum(2 * w + h, False, 0)
        if step == 0:
            for w in range(GROUP):
                norm_sums[0, w] = lane_fold(square_sum(firsts[w][...].astype(F32)))
            norm_pair = pair(5, norm_sums.at[0], norm_sums.at[1])
            norm_pair.start()
        turn = ring // 2 - 1
        ordered = [2 * w + h for w in order for h in range(LANE_PARTS)]
        for s in range(turn):
            for flow in ordered:
                far, back = reach(flow % LANE_PARTS)
                if s < far - 1:
                    pass_sum(flow, True, s)
                if s < back - 1:
                    pass_sum(flow, False, s)
        for flow in ordered:
            far, back = reach(flow % LANE_PARTS)
            w, h = flows[flow]
            at = chunk(place)
            copies[flow, far - 1].wait_recv()
            copies[flow, ring - 2].wait_recv()
            total = grads[flow, at, :].astype(F32) + arrived[flow, far - 1].astype(F32)
            total = total + arrived[flow, ring - 2].astype(F32)
            if step == 0:
                lanes = slice(h * 128, (h + 1) * 128)
                moved = firsts[w][at, lanes].astype(F32) + total
            else:
                moved = kept[flow] * scales[w] + total
            kept[flow] = moved
            rounded = moved.astype(BF16)
            blocks[flow, at, :] = rounded
            send_block(flow, True, 0)
            send_block(flow, False, 0)
            if step == STEPS - 1 and w == 2:
                send_w2(flow, place)
            part = square_sum(rounded.astype(F32))
            tally[0, w] = part if h == 0 else tally[0, w] + part
        tallies = []

        def start_tally(stage):
            copy = remote(
                tally.at[stage], tally_in.at[step * bits + stage],
                tally_send.at[stage], tally_recv.at[step * bits + stage],
                tally_partners[stage],
            )
            copy.start()
            tallies.append(copy)

        def end_tally(stage):
            tallies[stage].wait_recv()
            tally[stage + 1] = tally[stage] + tally_in[step * bits + stage]
            if stage + 1 < bits:
                start_tally(stage + 1)

        start_tally(0)
        ended = 0
        for t in range(turn + 1):
            for w in order:
                for h in range(LANE_PARTS):
                    flow = 2 * w + h
                    far, back = reach(h)
                    for to_right, count in ((True, far), (False, back)):
                        if t >= count:
                            continue
                        copies[flow, ring - 1 + (t if to_right else far + t)].wait_recv()
                        if t < count - 1:
                            send_block(flow, to_right, t + 1)
                        if step == STEPS - 1 and w == 2:
                            send_w2(flow, place + (ring - 1 - t if to_right else 1 + t))
                if t == turn:
                    if step < STEPS - 1:
                        source = us if w == 2 else ks
                        act_dot(1, w, source, own)
                        act_dot(1, w, source, other)
                    elif w == 2:
                        w2_pair = pair(6, blocks.at[4:6], near_w2)
                        w2_pair.start()
                    else:
                        if w == 0:
                            q_pair.wait_recv()
                            loads[5].wait()
                        act_dot(1, w, qs, own)
                        act_dot(1, w, qs, other)
            if t < turn and ended < bits:
                end_tally(ended)
                ended += 1
        while ended < bits:
            end_tally(ended)
            ended += 1
        if step == 0:
            norm_pair.wait()
            norms = [
                jnp.sqrt(jnp.sum(norm_sums[0, w] + norm_sums[1, w], keepdims=True))
                for w in range(GROUP)
            ]
        for copy in list(copies.values()) + tallies:
            copy.wait_send()
        scales = [
            norms[w] / jnp.sqrt(jnp.sum(tally[bits, w], keepdims=True) + 1e-06)
            for w in range(GROUP)
        ]

    tile = tokens // TILES
    scale_out[...] = jnp.broadcast_to(scales[2], scale_out.shape)
    scale_swap = remote(
        scale_out, far_scale, side_send.at[1], side_recv.at[1], across
    )
    scale_swap.start()
    hid_copies = []

    def send_hid(slot, source, target, device):
        copy = remote(source, target, hid_send.at[slot], hid_recv.at[slot], device)
        copy.start()
        return copy

    for t in range(TILES):
        trio = []
        for side in range(CORES):
            at = slice(side * tokens + t * tile, side * tokens + (t + 1) * tile)
            act = acts[0, at, :] * scales[0]
            lin = acts[1, at, :] * scales[1]
            hq[at, :] = (act * jax.nn.sigmoid(act) * lin).astype(BF16)
            to = slice(t * tile, (t + 1) * tile)
            if side == 0:
                trio.append(send_hid(3 * t, hq.at[at, :], far_hid.at[0, to, :], across))
            else:
                trio.append(
                    send_hid(3 * t + 1, hq.at[at, :], far_hid.at[1, to, :], diagonal)
                )
                trio.append(send_hid(3 * t + 2, hq.at[at, :], near_hid.at[to, :], sibling))
        hid_copies.append(trio)
    w_swap.wait()
    w_share = pair(7, w_far.at[own_rows, :], w_far.at[own_rows, :])
    w_share.start()
    w2_pair.wait()
    own_w2 = jnp.concatenate([blocks[4], blocks[5]], axis=1)
    wide = ((1,), (1,))
    for t in range(TILES):
        at = slice(t * tile, (t + 1) * tile)
        hid_copies[t][2].wait_recv()
        mine = dot(hq[at, :], own_w2, wide)
        theirs = dot(
            near_hid[at, :], jnp.concatenate([near_w2[0], near_w2[1]], axis=1), wide
        )
        near[at, :] = ((mine + theirs) * scales[2]).astype(BF16)
    for copy in w2_copies:
        copy.wait()
    far_pair = pair(8, far_w2.at[0:2], far_w2.at[2:4])
    far_pair.start()
    w_copy.wait()
    stripe = half // 5

    def near_cols_of(c, carry):
        lanes = pl.ds(pl.multiple_of(c * stripe, 128), stripe)
        total_out[:, lanes] = dot(near[...], w_near[:, lanes])
        return carry

    lax.fori_loop(0, 5, near_cols_of, 0)
    scale_swap.wait()
    far_pair.wait()
    w_share.wait()
    scale = jnp.max(far_scale[...], keepdims=True)
    for t in range(TILES):
        at = slice(t * tile, (t + 1) * tile)
        hid_copies[t][0].wait_recv()
        hid_copies[t][1].wait_recv()
        mine = dot(
            far_hid[0, at, :], jnp.concatenate([far_w2[0], far_w2[1]], axis=1), wide
        )
        theirs = dot(
            far_hid[1, at, :], jnp.concatenate([far_w2[2], far_w2[3]], axis=1), wide
        )
        near[at, :] = ((mine + theirs) * scale).astype(BF16)

        def far_cols_of(c, carry):
            lanes = pl.ds(pl.multiple_of(c * stripe, 128), stripe)
            added = total_out[at, lanes] + dot(near[at, :], w_far[:, lanes])
            out[at, lanes] = added.astype(BF16)
            return carry

        lax.fori_loop(0, 5, far_cols_of, 0)
    for trio in hid_copies:
        for copy in trio:
            copy.wait_send()
    for copy in (k_pair, u_pair, kt_pair, ut_pair, q_pair):
        copy.wait_send()


def shards(n_ctx, queries, keys, values, rates, w_up, w_gate, w_down, w_out):
    tokens, rows = keys.shape
    cols = w_up.shape[2] // CORES
    half = w_out.shape[1] // 2
    ring = n_ctx // CORES
    size = rows // ring
    bits = n_ctx.bit_length() - 1
    flows = GROUP * LANE_PARTS
    vmem = pl.BlockSpec(memory_space=pltpu.VMEM)
    anywhere = pl.BlockSpec(memory_space=pl.ANY)
    dma = pltpu.SemaphoreType.DMA
    return pl.pallas_call(
        functools.partial(layer_kernel, n_ctx),
        out_shape=jax.ShapeDtypeStruct((tokens, half), BF16),
        in_specs=[anywhere] * 3 + [vmem] + [anywhere] * 4,
        out_specs=vmem,
        scratch_shapes=[
            pltpu.VMEM((2 * tokens, rows), BF16),
            pltpu.VMEM((2 * tokens, rows), BF16),
            pltpu.VMEM((2 * tokens, rows), BF16),
            pltpu.VMEM((tokens, rows), BF16),
            pltpu.VMEM((rows, 2 * tokens), BF16),
            pltpu.VMEM((rows, 2 * tokens), BF16),
            pltpu.VMEM((rows, cols), BF16),
            pltpu.VMEM((rows, cols), BF16),
            pltpu.VMEM((cols, rows), BF16),
            pltpu.VMEM((rows, cols), BF16),
            pltpu.VMEM((GROUP, 2 * tokens, cols), F32),
            pltpu.VMEM((GROUP, 2 * tokens, cols), BF16),
            pltpu.VMEM((flows, rows, cols // LANE_PARTS), BF16),
            pltpu.VMEM((flows, rows, cols // LANE_PARTS), BF16),
            pltpu.VMEM((flows, ring - 1, size, cols // LANE_PARTS), BF16),
            pltpu.VMEM((flows, size, cols // LANE_PARTS), F32),
            pltpu.VMEM((bits + 1, GROUP, 8, 128), F32),
            pltpu.VMEM((STEPS * bits, GROUP, 8, 128), F32),
            pltpu.VMEM((CORES, GROUP, 8, 128), F32),
            pltpu.VMEM((2 * tokens, cols), BF16),
            pltpu.VMEM((tokens, cols), BF16),
            pltpu.VMEM((CORES, tokens, cols), BF16),
            pltpu.VMEM((LANE_PARTS, rows, cols // LANE_PARTS), BF16),
            pltpu.VMEM((CORES * LANE_PARTS, rows, cols // LANE_PARTS), BF16),
            pltpu.VMEM((8, 128), F32),
            pltpu.VMEM((8, 128), F32),
            pltpu.VMEM((rows, half), BF16),
            pltpu.VMEM((rows, half), BF16),
            pltpu.VMEM((tokens, rows), BF16),
            pltpu.VMEM((tokens, half), F32),
            dma((flows, 2 * (ring - 1))),
            dma((flows, 2 * (ring - 1))),
            dma((9,)),
            dma((9,)),
            dma((bits,)),
            dma((STEPS * bits,)),
            dma((2,)),
            dma((2,)),
            dma((LANE_PARTS * ring,)),
            dma((LANE_PARTS * ring,)),
            dma((3 * TILES,)),
            dma((3 * TILES,)),
            dma((7,)),
        ],
        compiler_params=pltpu.CompilerParams(
            collective_id=0, has_side_effects=True, vmem_limit_bytes=60 << 20
        ),
    )(queries, keys, values, rates.T, w_up[0], w_gate[0], w_down[0], w_out)


def solution(mesh):
    def body(*args):
        return shards(mesh.shape["ctx"], *args)

    return jax.shard_map(
        body,
        mesh=mesh,
        in_specs=(
            P("ctx", "head"),
            P("ctx", "head"),
            P("ctx", "head"),
            P("ctx", "head"),
            P("head", None, None),
            P("head", None, None),
            P("head", None, None),
            P("head", None),
        ),
        out_specs=P("ctx", "head"),
        check_vma=False,
    )
```

time: 143 us -> 107 us (0.75)
  Pallas kernels: 138 us -> 103 us
  local copies, waits for them, and re-layouts: 4.93 us -> 3.4 us
    pallas_call x1, Pallas kernels: 138 us -> 103 us  [shards(): pl.pallas_call(functools.partial(layer_kernel, n_ctx), out_shape=jax.Shap...]
    unnamed x2 -> x1, local copies, waits for them, and re-layouts: 4.93 us -> 3.4 us
where the time goes in v1:
time: 107 us; the launch traced here: 106 us
  Pallas kernels  103 us (96%)
  local copies, waits for them, and re-layouts  3.4 us (3%)
    pallas_call x1, Pallas kernels, shards(): pl.pallas_call(functools.partial(layer_kernel, n_ctx), out_shape=jax.Shap...  103 us
    unnamed x1, local copies, waits for them, and re-layouts  3.4 us

profile of v1, /device:TPU:0, one launch (start us, length us, event | category | flops | bytes accessed | tf_op | source)
XLA Modules:
  0.0 106.1 jit_solution(12371624571531512174)
XLA Ops:
  0.0 102.7 %shard_map.82 = bf16[512,2560]{1,0:T(8,128)(2,1)} custom-call(bf16[512,1024]{1,0:T(8,128)(2,1)} %q.1, bf16[512,1024]{1,0:T(8,128)(2,1)} %k.1, bf16[512,1024]{1,0:T(8,128)(2,1)} %v.1, f32[1,512]{1,0:T(1,128)} %bitcast.7, bf16[1024,512]{1,0:T(8,128)(2,1)} %bitcast.4, bf16[1024,512]{1,0:T(8,128)(2,1)} %bitcast.5, bf16[512,1024]{1,0:T(8,128)(2,1)} %bitcast.6, ...), custom_call_target="tpu_custom_call" | custom-call | tf_op jit(solution)/shard_map/pallas_call | solution.py:460
  102.7 3.4 %copy.10 = bf16[512,2560]{1,0:T(8,128)(2,1)} copy(bf16[512,2560]{1,0:T(8,128)(2,1)} %shard_map.82) | data formatting | bytes 5242880

commit v2 on v1

--- a/solution.py
+++ b/solution.py
@@ -15,8 +15,10 @@
 LANE_PARTS = 2
 CORES = 2
 RING_ROWS = 4
-TILES = 4
-ORDERS = ((0, 1, 2), (2, 0, 1))
+TILES = 2
+PIECES = 4
+STRIPES = 5
+FIRST_SENT = (2, 0, 1)
 
 
 def ring_place(chip, width):
@@ -51,9 +53,9 @@
         ks, us, qs, vin, kt, ut, first0, first1, in2, first2,
         acts, mid, grads, blocks, arrived, kept, tally, tally_in, norm_sums,
         hq, near_hid, far_hid, near_w2, far_w2, far_scale, scale_out,
-        w_near, w_far, near, total_out,
+        w_near, w_far, near, total_out, staged,
         ring_send, ring_recv, pair_send, pair_recv, tally_send, tally_recv,
-        side_send, side_recv, w2_send, w2_recv, hid_send, hid_recv, local_sem,
+        side_send, side_recv, w2_send, w2_recv, hid_send, hid_recv, local_sem, out_sem,
     ) = scratch
     tokens, rows = k.shape
     cols = first0.shape[1]
@@ -133,15 +135,15 @@
         ut[at, own] = scaled.T
     u_pair = pair(1, us.at[own, :], us.at[other, :])
     u_pair.start()
+
+    def turned(source, target, side):
+        for t in range(rows // 128):
+            at = slice(t * 128, (t + 1) * 128)
+            target[at, side] = source[side, at].T
+
     loads[0].wait()
-    for t in range(rows // 128):
-        at = slice(t * 128, (t + 1) * 128)
-        kt[at, own] = ks[own, at].T
-    kt_pair = pair(2, kt.at[:, own], kt.at[:, other])
-    kt_pair.start()
-    ut_pair = pair(3, ut.at[:, own], ut.at[:, other])
-    ut_pair.start()
-    q_pair = pair(4, q, qs.at[other, :])
+    turned(ks, kt, own)
+    q_pair = pair(2, q, qs.at[other, :])
     q_pair.start()
     w_copy = local(6, w_out.at[:, near_cols], w_near)
     w_copy.start()
@@ -163,13 +165,40 @@
         product = dot(source[at, :], weight(step, w))
         acts[w, at, :] = product
 
-    for w, source in enumerate((ks, ks, us)):
-        act_dot(0, w, source, own)
+    act_dot(0, 0, ks, own)
+    act_dot(0, 1, ks, own)
     k_pair.wait_recv()
-    for w in range(2):
-        act_dot(0, w, ks, other)
-    u_pair.wait_recv()
-    act_dot(0, 2, us, other)
+    act_dot(0, 0, ks, other)
+    act_dot(0, 1, ks, other)
+    turned(ks, kt, other)
+
+    pieces = 2 * tokens // 128
+
+    def hid_gates(by):
+        def one(piece, carry):
+            at = pl.ds(pl.multiple_of(piece * 128, 128), 128)
+            act, lin = acts[0, at, :], acts[1, at, :]
+            if by[0] is not None:
+                act, lin = act * by[0], lin * by[1]
+            mid[2, at, :] = (act * jax.nn.sigmoid(act) * lin).astype(BF16)
+            return carry
+
+        lax.fori_loop(0, pieces, one, 0)
+
+    def err_gates(by):
+        def one(piece, carry):
+            at = pl.ds(pl.multiple_of(piece * 128, 128), 128)
+            act, lin, err = acts[0, at, :], acts[1, at, :], acts[2, at, :]
+            if by[0] is not None:
+                act, lin, err = act * by[0], lin * by[1], err * by[2]
+            sig = jax.nn.sigmoid(act)
+            mid[0, at, :] = (err * lin * sig * (1.0 + act * (1.0 - sig))).astype(BF16)
+            mid[1, at, :] = (err * (act * sig)).astype(BF16)
+            return carry
+
+        lax.fori_loop(0, pieces, one, 0)
+
+    hid_gates(scales)
 
     flows = [(w, h) for w in range(GROUP) for h in range(LANE_PARTS)]
 
@@ -180,26 +209,8 @@
     def chunk(number):
         return pl.ds(pl.multiple_of((number % ring) * size, size), size)
 
+    copies = {}
     for step in range(STEPS):
-        order = ORDERS[step % 2]
-        copies = {}
-
-        def gates(piece, carry):
-            at = pl.ds(pl.multiple_of(piece * 128, 128), 128)
-            act, lin, err = acts[0, at, :], acts[1, at, :], acts[2, at, :]
-            if step > 0:
-                act, lin, err = act * scales[0], lin * scales[1], err * scales[2]
-            sig = jax.nn.sigmoid(act)
-            gate = act * sig
-            mid[0, at, :] = (err * lin * sig * (1.0 + act * (1.0 - sig))).astype(BF16)
-            mid[1, at, :] = (err * gate).astype(BF16)
-            mid[2, at, :] = (gate * lin).astype(BF16)
-            return carry
-
-        lax.fori_loop(0, 2 * tokens // 128, gates, 0)
-        if step == 0:
-            kt_pair.wait_recv()
-            ut_pair.wait_recv()
 
         def send(flow, slot, source, target, device):
             copy = remote(
@@ -245,27 +256,37 @@
             copy.start()
             w2_copies.append(copy)
 
-        for w in order:
+        def grad(w):
             source = ut if w == 2 else kt
 
             def grad_rows(piece, carry):
-                at = pl.ds(pl.multiple_of(piece * (rows // 4), rows // 4), rows // 4)
+                at = pl.ds(pl.multiple_of(piece * (rows // PIECES), rows // PIECES), rows // PIECES)
                 product = dot(source[at, :], mid[w]).astype(BF16)
                 grads[2 * w, at, :] = product[:, :128]
                 grads[2 * w + 1, at, :] = product[:, 128:]
                 return carry
 
-            lax.fori_loop(0, 4, grad_rows, 0)
+            lax.fori_loop(0, PIECES, grad_rows, 0)
             for h in range(LANE_PARTS):
                 send_sum(2 * w + h, True, 0)
                 send_sum(2 * w + h, False, 0)
+
+        if step == 0:
+            u_pair.wait_recv()
+            turned(us, ut, other)
+            grad(2)
+            act_dot(0, 2, us, own)
+            act_dot(0, 2, us, other)
+        err_gates(scales)
+        grad(0)
+        grad(1)
         if step == 0:
             for w in range(GROUP):
                 norm_sums[0, w] = lane_fold(square_sum(firsts[w][...].astype(F32)))
-            norm_pair = pair(5, norm_sums.at[0], norm_sums.at[1])
+            norm_pair = pair(3, norm_sums.at[0], norm_sums.at[1])
             norm_pair.start()
         turn = ring // 2 - 1
-        ordered = [2 * w + h for w in order for h in range(LANE_PARTS)]
+        ordered = [2 * w + h for w in range(GROUP) for h in range(LANE_PARTS)]
         for s in range(turn):
             for flow in ordered:
                 far, back = reach(flow % LANE_PARTS)
@@ -312,53 +333,60 @@
             if stage + 1 < bits:
                 start_tally(stage + 1)
 
+        def take_block(flow, t):
+            far, back = reach(flow % LANE_PARTS)
+            for to_right, count in ((True, far), (False, back)):
+                if t >= count:
+                    continue
+                copies[flow, ring - 1 + (t if to_right else far + t)].wait_recv()
+                if t < count - 1:
+                    send_block(flow, to_right, t + 1)
+                if step == STEPS - 1 and flow // LANE_PARTS == 2:
+                    send_w2(flow, place + (ring - 1 - t if to_right else 1 + t))
+
         start_tally(0)
         ended = 0
-        for t in range(turn + 1):
-            for w in order:
-                for h in range(LANE_PARTS):
-                    flow = 2 * w + h
-                    far, back = reach(h)
-                    for to_right, count in ((True, far), (False, back)):
-                        if t >= count:
-                            continue
-                        copies[flow, ring - 1 + (t if to_right else far + t)].wait_recv()
-                        if t < count - 1:
-                            send_block(flow, to_right, t + 1)
-                        if step == STEPS - 1 and w == 2:
-                            send_w2(flow, place + (ring - 1 - t if to_right else 1 + t))
-                if t == turn:
-                    if step < STEPS - 1:
-                        source = us if w == 2 else ks
-                        act_dot(1, w, source, own)
-                        act_dot(1, w, source, other)
-                    elif w == 2:
-                        w2_pair = pair(6, blocks.at[4:6], near_w2)
-                        w2_pair.start()
-                    else:
-                        if w == 0:
-                            q_pair.wait_recv()
-                            loads[5].wait()
-                        act_dot(1, w, qs, own)
-                        act_dot(1, w, qs, other)
-            if t < turn and ended < bits:
-                end_tally(ended)
-                ended += 1
-        while ended < bits:
-            end_tally(ended)
-            ended += 1
+        for t in range(turn):
+            for flow in ordered:
+                take_block(flow, t)
+                if flow == ordered[3] and ended < bits - 1:
+                    end_tally(ended)
+                    ended += 1
         if step == 0:
             norm_pair.wait()
             norms = [
                 jnp.sqrt(jnp.sum(norm_sums[0, w] + norm_sums[1, w], keepdims=True))
                 for w in range(GROUP)
             ]
-        for copy in list(copies.values()) + tallies:
-            copy.wait_send()
+        else:
+            q_pair.wait_recv()
+            loads[5].wait()
+        source = ks if step == 0 else qs
+        for w in range(2):
+            for h in range(LANE_PARTS):
+                take_block(2 * w + h, turn)
+            act_dot(1, w, source, own)
+            act_dot(1, w, source, other)
+        while ended < bits:
+            end_tally(ended)
+            ended += 1
         scales = [
             norms[w] / jnp.sqrt(jnp.sum(tally[bits, w], keepdims=True) + 1e-06)
             for w in range(GROUP)
         ]
+        for (flow, slot), copy in copies.items():
+            if slot < ring - 1:
+                copy.wait_send()
+        old = {key: copy for key, copy in copies.items() if key[1] >= ring - 1}
+        if step == 0:
+            hid_gates(scales)
+            grad(2)
+            for h in range(LANE_PARTS):
+                take_block(4 + h, turn)
+            act_dot(1, 2, us, own)
+            act_dot(1, 2, us, other)
+        for copy in list(old.values()) + tallies:
+            copy.wait_send()
 
     tile = tokens // TILES
     scale_out[...] = jnp.broadcast_to(scales[2], scale_out.shape)
@@ -373,7 +401,7 @@
         copy.start()
         return copy
 
-    for t in range(TILES):
+    def send_tile(t):
         trio = []
         for side in range(CORES):
             at = slice(side * tokens + t * tile, side * tokens + (t + 1) * tile)
@@ -389,8 +417,17 @@
                 )
                 trio.append(send_hid(3 * t + 2, hq.at[at, :], near_hid.at[to, :], sibling))
         hid_copies.append(trio)
+
+    for t in range(TILES // 2):
+        send_tile(t)
+    for h in range(LANE_PARTS):
+        take_block(4 + h, turn)
+    w2_pair = pair(4, blocks.at[4:6], near_w2)
+    w2_pair.start()
+    for t in range(TILES // 2, TILES):
+        send_tile(t)
     w_swap.wait()
-    w_share = pair(7, w_far.at[own_rows, :], w_far.at[own_rows, :])
+    w_share = pair(5, w_far.at[own_rows, :], w_far.at[own_rows, :])
     w_share.start()
     w2_pair.wait()
     own_w2 = jnp.concatenate([blocks[4], blocks[5]], axis=1)
@@ -405,21 +442,26 @@
         near[at, :] = ((mine + theirs) * scales[2]).astype(BF16)
     for copy in w2_copies:
         copy.wait()
-    far_pair = pair(8, far_w2.at[0:2], far_w2.at[2:4])
+    far_pair = pair(6, far_w2.at[0:2], far_w2.at[2:4])
     far_pair.start()
     w_copy.wait()
-    stripe = half // 5
+    stripe = half // STRIPES
 
     def near_cols_of(c, carry):
         lanes = pl.ds(pl.multiple_of(c * stripe, 128), stripe)
         total_out[:, lanes] = dot(near[...], w_near[:, lanes])
         return carry
 
-    lax.fori_loop(0, 5, near_cols_of, 0)
+    lax.fori_loop(0, STRIPES, near_cols_of, 0)
     scale_swap.wait()
     far_pair.wait()
     w_share.wait()
     scale = jnp.max(far_scale[...], keepdims=True)
+
+    def out_copy(t, at, lanes, c):
+        here = staged.at[at, lanes]
+        return pltpu.make_async_copy(here, out.at[at, lanes], out_sem.at[t * STRIPES + c])
+
     for t in range(TILES):
         at = slice(t * tile, (t + 1) * tile)
         hid_copies[t][0].wait_recv()
@@ -435,14 +477,24 @@
         def far_cols_of(c, carry):
             lanes = pl.ds(pl.multiple_of(c * stripe, 128), stripe)
             added = total_out[at, lanes] + dot(near[at, :], w_far[:, lanes])
-            out[at, lanes] = added.astype(BF16)
+            staged[at, lanes] = added.astype(BF16)
+            out_copy(t, at, lanes, c).start()
             return carry
 
-        lax.fori_loop(0, 5, far_cols_of, 0)
+        lax.fori_loop(0, STRIPES, far_cols_of, 0)
+    for t in range(TILES):
+        at = slice(t * tile, (t + 1) * tile)
+
+        def written(c, carry):
+            lanes = pl.ds(pl.multiple_of(c * stripe, 128), stripe)
+            out_copy(t, at, lanes, c).wait()
+            return carry
+
+        lax.fori_loop(0, STRIPES, written, 0)
     for trio in hid_copies:
         for copy in trio:
             copy.wait_send()
-    for copy in (k_pair, u_pair, kt_pair, ut_pair, q_pair):
+    for copy in (k_pair, u_pair, q_pair):
         copy.wait_send()
 
 
@@ -461,7 +513,7 @@
         functools.partial(layer_kernel, n_ctx),
         out_shape=jax.ShapeDtypeStruct((tokens, half), BF16),
         in_specs=[anywhere] * 3 + [vmem] + [anywhere] * 4,
-        out_specs=vmem,
+        out_specs=anywhere,
         scratch_shapes=[
             pltpu.VMEM((2 * tokens, rows), BF16),
             pltpu.VMEM((2 * tokens, rows), BF16),
@@ -493,10 +545,11 @@
             pltpu.VMEM((rows, half), BF16),
             pltpu.VMEM((tokens, rows), BF16),
             pltpu.VMEM((tokens, half), F32),
+            pltpu.VMEM((tokens, half), BF16),
             dma((flows, 2 * (ring - 1))),
             dma((flows, 2 * (ring - 1))),
-            dma((9,)),
-            dma((9,)),
+            dma((7,)),
+            dma((7,)),
             dma((bits,)),
             dma((STEPS * bits,)),
             dma((2,)),
@@ -506,6 +559,7 @@
             dma((3 * TILES,)),
             dma((3 * TILES,)),
             dma((7,)),
+            dma((TILES * STRIPES,)),
         ],
         compiler_params=pltpu.CompilerParams(
             collective_id=0, has_side_effects=True, vmem_limit_bytes=60 << 20

time: 107 us -> 108 us (level)
    pallas_call x1, Pallas kernels: 103 us -> 104 us  [shards(): pl.pallas_call(functools.partial(layer_kernel, n_ctx), out_shape=jax.Shap...]
where the time goes in v2:
time: 108 us; the launch traced here: 107 us
  Pallas kernels  104 us (96%)
  local copies, waits for them, and re-layouts  3.4 us (3%)
    pallas_call x1, Pallas kernels, shards(): pl.pallas_call(functools.partial(layer_kernel, n_ctx), out_shape=jax.Shap...  104 us
    unnamed x1, local copies, waits for them, and re-layouts  3.4 us

profile of v2, /device:TPU:0, one launch (start us, length us, event | category | flops | bytes accessed | tf_op | source)
XLA Modules:
  0.0 107.5 jit_solution(3850204959654505523)
XLA Ops:
  0.0 104.1 %shard_map.82 = bf16[512,2560]{1,0:T(8,128)(2,1)} custom-call(bf16[512,1024]{1,0:T(8,128)(2,1)} %q.1, bf16[512,1024]{1,0:T(8,128)(2,1)} %k.1, bf16[512,1024]{1,0:T(8,128)(2,1)} %v.1, f32[1,512]{1,0:T(1,128)} %bitcast.7, bf16[1024,512]{1,0:T(8,128)(2,1)} %bitcast.4, bf16[1024,512]{1,0:T(8,128)(2,1)} %bitcast.5, bf16[512,1024]{1,0:T(8,128)(2,1)} %bitcast.6, ...), custom_call_target="tpu_custom_call" | custom-call | tf_op jit(solution)/shard_map/pallas_call | solution.py:512
  104.1 3.4 %copy.10 = bf16[512,2560]{1,0:T(8,128)(2,1)} copy(bf16[512,2560]{1,0:T(8,128)(2,1)} %shard_map.82) | data formatting | bytes 5242880

commit v3 on v2

--- a/solution.py
+++ b/solution.py
@@ -15,9 +15,10 @@
 LANE_PARTS = 2
 CORES = 2
 RING_ROWS = 4
-TILES = 2
-PIECES = 4
+TILES = (4, 2, 2)
+PIECES = 2
 STRIPES = 5
+COPY_PIECES = 8
 FIRST_SENT = (2, 0, 1)
 
 
@@ -55,7 +56,7 @@
         hq, near_hid, far_hid, near_w2, far_w2, far_scale, scale_out,
         w_near, w_far, near, total_out, staged,
         ring_send, ring_recv, pair_send, pair_recv, tally_send, tally_recv,
-        side_send, side_recv, w2_send, w2_recv, hid_send, hid_recv, local_sem, out_sem,
+        side_send, side_recv, w2_send, w2_recv, near_send, near_recv, hid_send, hid_recv, local_sem, out_sem,
     ) = scratch
     tokens, rows = k.shape
     cols = first0.shape[1]
@@ -102,7 +103,7 @@
         local(4, w2.at[pl.ds(pl.multiple_of(core * cols, 128), cols), :], in2),
         local(5, q, qs.at[own, :]),
     ]
-    for load in loads:
+    for load in loads[:5]:
         load.start()
 
     partners = [right, left, sibling, across, diagonal] + tally_partners
@@ -116,6 +117,7 @@
 
     k_pair = pair(0, k, ks.at[other, :])
     k_pair.start()
+    loads[5].start()
     near_cols = pl.ds(pl.multiple_of(head * half, 128), half)
     far_cols = pl.ds(pl.multiple_of((1 - head) * half, 128), half)
     depth = rows // CORES
@@ -165,16 +167,13 @@
         product = dot(source[at, :], weight(step, w))
         acts[w, at, :] = product
 
-    act_dot(0, 0, ks, own)
-    act_dot(0, 1, ks, own)
-    k_pair.wait_recv()
-    act_dot(0, 0, ks, other)
-    act_dot(0, 1, ks, other)
-    turned(ks, kt, other)
-
-    pieces = 2 * tokens // 128
-
-    def hid_gates(by):
+    for w, source in enumerate((ks, ks, us)):
+        act_dot(0, w, source, own)
+
+    half_pieces = tokens // 128
+    whole = (0, 2 * half_pieces)
+
+    def hid_gates(by, span):
         def one(piece, carry):
             at = pl.ds(pl.multiple_of(piece * 128, 128), 128)
             act, lin = acts[0, at, :], acts[1, at, :]
@@ -183,9 +182,9 @@
             mid[2, at, :] = (act * jax.nn.sigmoid(act) * lin).astype(BF16)
             return carry
 
-        lax.fori_loop(0, pieces, one, 0)
-
-    def err_gates(by):
+        lax.fori_loop(*span, one, 0)
+
+    def err_gates(by, span):
         def one(piece, carry):
             at = pl.ds(pl.multiple_of(piece * 128, 128), 128)
             act, lin, err = acts[0, at, :], acts[1, at, :], acts[2, at, :]
@@ -196,9 +195,14 @@
             mid[1, at, :] = (err * (act * sig)).astype(BF16)
             return carry
 
-        lax.fori_loop(0, pieces, one, 0)
-
-    hid_gates(scales)
+        lax.fori_loop(*span, one, 0)
+
+    hid_gates(scales, (0, half_pieces))
+    err_gates(scales, (0, half_pieces))
+    k_pair.wait_recv()
+    act_dot(0, 0, ks, other)
+    act_dot(0, 1, ks, other)
+    hid_gates(scales, (half_pieces, 2 * half_pieces))
 
     flows = [(w, h) for w in range(GROUP) for h in range(LANE_PARTS)]
 
@@ -210,12 +214,16 @@
         return pl.ds(pl.multiple_of((number % ring) * size, size), size)
 
     copies = {}
+
+    def ring_sent(phase):
+        all_sent = grads.at[:, : (ring - 1) * size, :]
+        remote(all_sent, all_sent, ring_send.at[phase], ring_recv.at[0, 0], right).wait_send()
+
     for step in range(STEPS):
 
         def send(flow, slot, source, target, device):
-            copy = remote(
-                source, target, ring_send.at[flow, slot], ring_recv.at[flow, slot], device
-            )
+            phase = ring_send.at[0 if slot < ring - 1 else 1]
+            copy = remote(source, target, phase, ring_recv.at[flow, slot], device)
             copy.start()
             copies[flow, slot] = copy
 
@@ -243,30 +251,23 @@
             grads[flow, at, :] = total.astype(BF16)
             send_sum(flow, to_right, s + 1)
 
-        w2_copies = []
-
         def send_w2(flow, number):
-            h = flow % LANE_PARTS
             here = chunk(number)
-            slot = len(w2_copies)
-            copy = remote(
-                blocks.at[flow, here, :], far_w2.at[h, here, :],
-                w2_send.at[slot], w2_recv.at[slot], across,
-            )
-            copy.start()
-            w2_copies.append(copy)
+            target = far_w2.at[flow % LANE_PARTS, here, :]
+            remote(blocks.at[flow, here, :], target, w2_send, w2_recv, across).start()
+            target = near_w2.at[flow % LANE_PARTS, here, :]
+            remote(
+                blocks.at[flow, here, :], target, near_send, near_recv, sibling
+            ).start()
 
         def grad(w):
             source = ut if w == 2 else kt
 
-            def grad_rows(piece, carry):
-                at = pl.ds(pl.multiple_of(piece * (rows // PIECES), rows // PIECES), rows // PIECES)
+            for piece in range(PIECES):
+                at = slice(piece * (rows // PIECES), (piece + 1) * (rows // PIECES))
                 product = dot(source[at, :], mid[w]).astype(BF16)
                 grads[2 * w, at, :] = product[:, :128]
                 grads[2 * w + 1, at, :] = product[:, 128:]
-                return carry
-
-            lax.fori_loop(0, PIECES, grad_rows, 0)
             for h in range(LANE_PARTS):
                 send_sum(2 * w + h, True, 0)
                 send_sum(2 * w + h, False, 0)
@@ -275,9 +276,11 @@
             u_pair.wait_recv()
             turned(us, ut, other)
             grad(2)
-            act_dot(0, 2, us, own)
             act_dot(0, 2, us, other)
-        err_gates(scales)
+            err_gates(scales, (half_pieces, 2 * half_pieces))
+            turned(ks, kt, other)
+        else:
+            err_gates(scales, whole)
         grad(0)
         grad(1)
         if step == 0:
@@ -374,21 +377,20 @@
             norms[w] / jnp.sqrt(jnp.sum(tally[bits, w], keepdims=True) + 1e-06)
             for w in range(GROUP)
         ]
-        for (flow, slot), copy in copies.items():
-            if slot < ring - 1:
-                copy.wait_send()
-        old = {key: copy for key, copy in copies.items() if key[1] >= ring - 1}
+        ring_sent(0)
         if step == 0:
-            hid_gates(scales)
+            hid_gates(scales, whole)
             grad(2)
             for h in range(LANE_PARTS):
                 take_block(4 + h, turn)
             act_dot(1, 2, us, own)
             act_dot(1, 2, us, other)
-        for copy in list(old.values()) + tallies:
+        ring_sent(1)
+        for copy in tallies:
             copy.wait_send()
 
-    tile = tokens // TILES
+    ends = [tokens * sum(TILES[: t + 1]) // sum(TILES) for t in range(len(TILES))]
+    tiles = [(end - tokens * part // sum(TILES), end) for end, part in zip(ends, TILES)]
     scale_out[...] = jnp.broadcast_to(scales[2], scale_out.shape)
     scale_swap = remote(
         scale_out, far_scale, side_send.at[1], side_recv.at[1], across
@@ -397,73 +399,65 @@
     hid_copies = []
 
     def send_hid(slot, source, target, device):
-        copy = remote(source, target, hid_send.at[slot], hid_recv.at[slot], device)
+        copy = remote(source, target, hid_send, hid_recv.at[slot], device)
         copy.start()
         return copy
 
+    def hidden_of(side, first, last):
+        at = slice(side * tokens + first, side * tokens + last)
+        act = acts[0, at, :] * scales[0]
+        lin = acts[1, at, :] * scales[1]
+        hq[at, :] = (act * jax.nn.sigmoid(act) * lin).astype(BF16)
+
     def send_tile(t):
-        trio = []
-        for side in range(CORES):
-            at = slice(side * tokens + t * tile, side * tokens + (t + 1) * tile)
-            act = acts[0, at, :] * scales[0]
-            lin = acts[1, at, :] * scales[1]
-            hq[at, :] = (act * jax.nn.sigmoid(act) * lin).astype(BF16)
-            to = slice(t * tile, (t + 1) * tile)
-            if side == 0:
-                trio.append(send_hid(3 * t, hq.at[at, :], far_hid.at[0, to, :], across))
-            else:
-                trio.append(
-                    send_hid(3 * t + 1, hq.at[at, :], far_hid.at[1, to, :], diagonal)
-                )
-                trio.append(send_hid(3 * t + 2, hq.at[at, :], near_hid.at[to, :], sibling))
-        hid_copies.append(trio)
-
-    for t in range(TILES // 2):
-        send_tile(t)
+        first, last = tiles[t]
+        to, at = slice(first, last), slice(tokens + first, tokens + last)
+        hid_copies.append((
+            send_hid(2 * t, hq.at[to, :], far_hid.at[0, to, :], across),
+            send_hid(2 * t + 1, hq.at[at, :], far_hid.at[1, to, :], diagonal),
+        ))
+
     for h in range(LANE_PARTS):
         take_block(4 + h, turn)
-    w2_pair = pair(4, blocks.at[4:6], near_w2)
-    w2_pair.start()
-    for t in range(TILES // 2, TILES):
-        send_tile(t)
+    for side in range(CORES):
+        hidden_of(side, *tiles[0])
+    send_tile(0)
+    for side in (1, 0):
+        hidden_of(side, tiles[1][0], tokens)
+    near_copy = send_hid(2 * len(TILES), hq.at[other, :], near_hid, sibling)
+    send_tile(1)
     w_swap.wait()
-    w_share = pair(5, w_far.at[own_rows, :], w_far.at[own_rows, :])
+    w_share = pair(4, w_far.at[own_rows, :], w_far.at[own_rows, :])
     w_share.start()
-    w2_pair.wait()
-    own_w2 = jnp.concatenate([blocks[4], blocks[5]], axis=1)
     wide = ((1,), (1,))
-    for t in range(TILES):
-        at = slice(t * tile, (t + 1) * tile)
-        hid_copies[t][2].wait_recv()
-        mine = dot(hq[at, :], own_w2, wide)
-        theirs = dot(
-            near_hid[at, :], jnp.concatenate([near_w2[0], near_w2[1]], axis=1), wide
-        )
-        near[at, :] = ((mine + theirs) * scales[2]).astype(BF16)
-    for copy in w2_copies:
-        copy.wait()
-    far_pair = pair(6, far_w2.at[0:2], far_w2.at[2:4])
+    stripe = half // STRIPES
+
+    def near_stripes(first, last):
+        def one(c, carry):
+            lanes = pl.ds(pl.multiple_of(c * stripe, 128), stripe)
+            total_out[:, lanes] = dot(near[...], w_near[:, lanes])
+            return carry
+
+        lax.fori_loop(first, last, one, 0)
+
+    remote(near_w2, near_w2, near_send, near_recv, sibling).wait()
+    near_copy.wait_recv()
+    mine = dot(hq[own, :], jnp.concatenate([blocks[4], blocks[5]], axis=1), wide)
+    theirs = dot(near_hid[...], jnp.concatenate([near_w2[0], near_w2[1]], axis=1), wide)
+    near[...] = ((mine + theirs) * scales[2]).astype(BF16)
+    send_tile(2)
+    w_copy.wait()
+    near_stripes(0, STRIPES - 2)
+    remote(far_w2.at[0:2], far_w2.at[0:2], w2_send, w2_recv, across).wait()
+    far_pair = pair(5, far_w2.at[0:2], far_w2.at[2:4])
     far_pair.start()
-    w_copy.wait()
-    stripe = half // STRIPES
-
-    def near_cols_of(c, carry):
-        lanes = pl.ds(pl.multiple_of(c * stripe, 128), stripe)
-        total_out[:, lanes] = dot(near[...], w_near[:, lanes])
-        return carry
-
-    lax.fori_loop(0, STRIPES, near_cols_of, 0)
+    near_stripes(STRIPES - 2, STRIPES)
     scale_swap.wait()
+    w_share.wait()
     far_pair.wait()
-    w_share.wait()
     scale = jnp.max(far_scale[...], keepdims=True)
-
-    def out_copy(t, at, lanes, c):
-        here = staged.at[at, lanes]
-        return pltpu.make_async_copy(here, out.at[at, lanes], out_sem.at[t * STRIPES + c])
-
-    for t in range(TILES):
-        at = slice(t * tile, (t + 1) * tile)
+    for t, (first, last) in enumerate(tiles):
+        at = slice(first, last)
         hid_copies[t][0].wait_recv()
         hid_copies[t][1].wait_recv()
         mine = dot(
@@ -478,24 +472,30 @@
             lanes = pl.ds(pl.multiple_of(c * stripe, 128), stripe)
             added = total_out[at, lanes] + dot(near[at, :], w_far[:, lanes])
             staged[at, lanes] = added.astype(BF16)
-            out_copy(t, at, lanes, c).start()
+            pltpu.make_async_copy(staged.at[at, lanes], out.at[at, lanes], out_sem).start()
             return carry
 
         lax.fori_loop(0, STRIPES, far_cols_of, 0)
-    for t in range(TILES):
-        at = slice(t * tile, (t + 1) * tile)
-
-        def written(c, carry):
-            lanes = pl.ds(pl.multiple_of(c * stripe, 128), stripe)
-            out_copy(t, at, lanes, c).wait()
-            return carry
-
-        lax.fori_loop(0, STRIPES, written, 0)
-    for trio in hid_copies:
-        for copy in trio:
-            copy.wait_send()
+    pltpu.make_async_copy(staged, out, out_sem).wait()
+    hid_sent = us.at[: (CORES + 1) * tokens * cols // rows, :]
+    remote(hid_sent, hid_sent, hid_send, hid_recv.at[0], sibling).wait_send()
     for copy in (k_pair, u_pair, q_pair):
         copy.wait_send()
+
+
+def copy_kernel(source, target, held, in_sem, out_sem):
+    rows = held.shape[0] // COPY_PIECES
+    pieces = [pl.ds(piece * rows, rows) for piece in range(COPY_PIECES)]
+    reads = [
+        pltpu.make_async_copy(source.at[at, :], held.at[at, :], in_sem.at[piece])
+        for piece, at in enumerate(pieces)
+    ]
+    for read in reads:
+        read.start()
+    for read, at in zip(reads, pieces):
+        read.wait()
+        pltpu.make_async_copy(held.at[at, :], target.at[at, :], out_sem).start()
+    pltpu.make_async_copy(held, target, out_sem).wait()
 
 
 def shards(n_ctx, queries, keys, values, rates, w_up, w_gate, w_down, w_out):
@@ -509,7 +509,7 @@
     vmem = pl.BlockSpec(memory_space=pltpu.VMEM)
     anywhere = pl.BlockSpec(memory_space=pl.ANY)
     dma = pltpu.SemaphoreType.DMA
-    return pl.pallas_call(
+    mixed = pl.pallas_call(
         functools.partial(layer_kernel, n_ctx),
         out_shape=jax.ShapeDtypeStruct((tokens, half), BF16),
         in_specs=[anywhere] * 3 + [vmem] + [anywhere] * 4,
@@ -546,25 +546,34 @@
             pltpu.VMEM((tokens, rows), BF16),
             pltpu.VMEM((tokens, half), F32),
             pltpu.VMEM((tokens, half), BF16),
+            dma((2,)),
             dma((flows, 2 * (ring - 1))),
-            dma((flows, 2 * (ring - 1))),
-            dma((7,)),
-            dma((7,)),
+            dma((6,)),
+            dma((6,)),
             dma((bits,)),
             dma((STEPS * bits,)),
             dma((2,)),
             dma((2,)),
-            dma((LANE_PARTS * ring,)),
-            dma((LANE_PARTS * ring,)),
-            dma((3 * TILES,)),
-            dma((3 * TILES,)),
+            dma,
+            dma,
+            dma,
+            dma,
+            dma,
+            dma((2 * len(TILES) + 1,)),
             dma((7,)),
-            dma((TILES * STRIPES,)),
+            dma,
         ],
         compiler_params=pltpu.CompilerParams(
             collective_id=0, has_side_effects=True, vmem_limit_bytes=60 << 20
         ),
     )(queries, keys, values, rates.T, w_up[0], w_gate[0], w_down[0], w_out)
+    return pl.pallas_call(
+        copy_kernel,
+        out_shape=jax.ShapeDtypeStruct((tokens, half), BF16),
+        in_specs=[anywhere],
+        out_specs=anywhere,
+        scratch_shapes=[pltpu.VMEM((tokens, half), BF16), dma((COPY_PIECES,)), dma],
+    )(mixed)
 
 
 def solution(mesh):

time: 108 us -> 100 us (0.926)
  Pallas kernels: 104 us -> 98.5 us
  local copies, waits for them, and re-layouts: 3.4 us -> 0 us
    pallas_call x1, Pallas kernels: 104 us -> 95.9 us  [shards(): pl.pallas_call(functools.partial(layer_kernel, n_ctx), out_shape=jax.Shap...]
    unnamed x1 -> x0, local copies, waits for them, and re-layouts: 3.4 us -> none
    pallas_call x0 -> x1, Pallas kernels: none -> 2.53 us  [shards(): pl.pallas_call(copy_kernel, out_shape=jax.ShapeDtypeStruct((tokens, half)...]
where the time goes in v3:
time: 100 us; the launch traced here: 98.5 us
  Pallas kernels  98.5 us (98%)
    pallas_call x1, Pallas kernels, shards(): pl.pallas_call(functools.partial(layer_kernel, n_ctx), out_shape=jax.Shap...  95.9 us
    pallas_call x1, Pallas kernels, shards(): pl.pallas_call(copy_kernel, out_shape=jax.ShapeDtypeStruct((tokens, half)...  2.53 us

profile of v3, /device:TPU:0, one launch (start us, length us, event | category | flops | bytes accessed | tf_op | source)
XLA Modules:
  0.0 98.5 jit_solution(13237740425050291839)
XLA Ops:
  0.0 95.9 %shard_map.82.source = bf16[512,2560]{1,0:T(8,128)(2,1)} custom-call(bf16[512,1024]{1,0:T(8,128)(2,1)} %q.1, bf16[512,1024]{1,0:T(8,128)(2,1)} %k.1, bf16[512,1024]{1,0:T(8,128)(2,1)} %v.1, f32[1,512]{1,0:T(1,128)} %bitcast.7, bf16[1024,512]{1,0:T(8,128)(2,1)} %bitcast.4, bf16[1024,512]{1,0:T(8,128)(2,1)} %bitcast.5, bf16[512,1024]{1,0:T(8,128)(2,1)} %bitcast.6, ...), custom_call_target="tpu_custom_call" | custom-call | tf_op jit(solution)/shard_map/pallas_call | solution.py:512
  95.9 2.5 %shard_map.83 = bf16[512,2560]{1,0:T(8,128)(2,1)} custom-call(bf16[512,2560]{1,0:T(8,128)(2,1)} %shard_map.82.source), custom_call_target="tpu_custom_call" | custom-call | tf_op jit(solution)/shard_map/pallas_call | solution.py:570

commit v4 on v3

--- a/solution.py
+++ b/solution.py
@@ -19,7 +19,6 @@
 PIECES = 2
 STRIPES = 5
 COPY_PIECES = 8
-FIRST_SENT = (2, 0, 1)
 
 
 def ring_place(chip, width):
@@ -355,6 +354,10 @@
                 if flow == ordered[3] and ended < bits - 1:
                     end_tally(ended)
                     ended += 1
+            if step == STEPS - 1 and t == turn // 2:
+                w_swap.wait()
+                w_share = pair(4, w_far.at[own_rows, :], w_far.at[own_rows, :])
+                w_share.start()
         if step == 0:
             norm_pair.wait()
             norms = [
@@ -417,18 +420,12 @@
             send_hid(2 * t + 1, hq.at[at, :], far_hid.at[1, to, :], diagonal),
         ))
 
+    for side in range(CORES):
+        hidden_of(side, 0, tokens)
     for h in range(LANE_PARTS):
         take_block(4 + h, turn)
-    for side in range(CORES):
-        hidden_of(side, *tiles[0])
+    near_copy = send_hid(2 * len(TILES), hq.at[other, :], near_hid, sibling)
     send_tile(0)
-    for side in (1, 0):
-        hidden_of(side, tiles[1][0], tokens)
-    near_copy = send_hid(2 * len(TILES), hq.at[other, :], near_hid, sibling)
-    send_tile(1)
-    w_swap.wait()
-    w_share = pair(4, w_far.at[own_rows, :], w_far.at[own_rows, :])
-    w_share.start()
     wide = ((1,), (1,))
     stripe = half // STRIPES
 
@@ -440,21 +437,24 @@
 
         lax.fori_loop(first, last, one, 0)
 
-    remote(near_w2, near_w2, near_send, near_recv, sibling).wait()
+    near_w2_copy = remote(near_w2, near_w2, near_send, near_recv, sibling)
+    near_w2_copy.wait_recv()
     near_copy.wait_recv()
     mine = dot(hq[own, :], jnp.concatenate([blocks[4], blocks[5]], axis=1), wide)
     theirs = dot(near_hid[...], jnp.concatenate([near_w2[0], near_w2[1]], axis=1), wide)
     near[...] = ((mine + theirs) * scales[2]).astype(BF16)
-    send_tile(2)
     w_copy.wait()
-    near_stripes(0, STRIPES - 2)
-    remote(far_w2.at[0:2], far_w2.at[0:2], w2_send, w2_recv, across).wait()
+    near_stripes(0, 2)
+    for t in range(1, len(TILES)):
+        send_tile(t)
+    far_w2_copy = remote(far_w2.at[0:2], far_w2.at[0:2], w2_send, w2_recv, across)
+    far_w2_copy.wait_recv()
     far_pair = pair(5, far_w2.at[0:2], far_w2.at[2:4])
     far_pair.start()
-    near_stripes(STRIPES - 2, STRIPES)
+    near_stripes(2, STRIPES)
     scale_swap.wait()
-    w_share.wait()
-    far_pair.wait()
+    w_share.wait_recv()
+    far_pair.wait_recv()
     scale = jnp.max(far_scale[...], keepdims=True)
     for t, (first, last) in enumerate(tiles):
         at = slice(first, last)
@@ -478,6 +478,10 @@
         lax.fori_loop(0, STRIPES, far_cols_of, 0)
     pltpu.make_async_copy(staged, out, out_sem).wait()
     hid_sent = us.at[: (CORES + 1) * tokens * cols // rows, :]
+    near_w2_copy.wait_send()
+    far_w2_copy.wait_send()
+    far_pair.wait_send()
+    w_share.wait_send()
     remote(hid_sent, hid_sent, hid_send, hid_recv.at[0], sibling).wait_send()
     for copy in (k_pair, u_pair, q_pair):
         copy.wait_send()

time: 100 us -> 99 us (0.990)
  no operation moved by 1% of the time
where the time goes in v4:
time: 99 us; the launch traced here: 98 us
  Pallas kernels  98 us (99%)
    pallas_call x1, Pallas kernels, shards(): pl.pallas_call(functools.partial(layer_kernel, n_ctx), out_shape=jax.Shap...  95.5 us
    pallas_call x1, Pallas kernels, shards(): pl.pallas_call(copy_kernel, out_shape=jax.ShapeDtypeStruct((tokens, half)...  2.53 us

profile of v4, /device:TPU:0, one launch (start us, length us, event | category | flops | bytes accessed | tf_op | source)
XLA Modules:
  0.0 98.0 jit_solution(11864201957356334714)
XLA Ops:
  0.0 95.5 %shard_map.82.source = bf16[512,2560]{1,0:T(8,128)(2,1)} custom-call(bf16[512,1024]{1,0:T(8,128)(2,1)} %q.1, bf16[512,1024]{1,0:T(8,128)(2,1)} %k.1, bf16[512,1024]{1,0:T(8,128)(2,1)} %v.1, f32[1,512]{1,0:T(1,128)} %bitcast.7, bf16[1024,512]{1,0:T(8,128)(2,1)} %bitcast.4, bf16[1024,512]{1,0:T(8,128)(2,1)} %bitcast.5, bf16[512,1024]{1,0:T(8,128)(2,1)} %bitcast.6, ...), custom_call_target="tpu_custom_call" | custom-call | tf_op jit(solution)/shard_map/pallas_call | solution.py:516
  95.5 2.5 %shard_map.83 = bf16[512,2560]{1,0:T(8,128)(2,1)} custom-call(bf16[512,2560]{1,0:T(8,128)(2,1)} %shard_map.82.source), custom_call_target="tpu_custom_call" | custom-call | tf_op jit(solution)/shard_map/pallas_call | solution.py:574

commit v5 on v4

--- a/solution.py
+++ b/solution.py
@@ -272,12 +272,12 @@
                 send_sum(2 * w + h, False, 0)
 
         if step == 0:
+            turned(ks, kt, other)
             u_pair.wait_recv()
             turned(us, ut, other)
             grad(2)
             act_dot(0, 2, us, other)
             err_gates(scales, (half_pieces, 2 * half_pieces))
-            turned(ks, kt, other)
         else:
             err_gates(scales, whole)
         grad(0)
@@ -346,11 +346,34 @@
                 if step == STEPS - 1 and flow // LANE_PARTS == 2:
                     send_w2(flow, place + (ring - 1 - t if to_right else 1 + t))
 
+        if step > 0:
+            q_pair.wait_recv()
+            loads[5].wait()
+        wanted = (ks, ks, us) if step == 0 else (qs, qs)
+
+        def pair_dot(w, one, two, fresh):
+            pair_at = (chunk(one), chunk(two))
+            right_side = jnp.concatenate(
+                [
+                    jnp.concatenate([blocks[2 * w, at, :], blocks[2 * w + 1, at, :]], axis=1)
+                    for at in pair_at
+                ],
+                axis=0,
+            )
+            for side in (own, other):
+                left_side = jnp.concatenate([wanted[w][side, at] for at in pair_at], axis=1)
+                product = dot(left_side, right_side)
+                acts[w, side, :] = product if fresh else acts[w, side, :] + product
+
+        in_pairs = size % 128 == 0
         start_tally(0)
         ended = 0
         for t in range(turn):
             for flow in ordered:
                 take_block(flow, t)
+                w, h = flows[flow]
+                if in_pairs and h == LANE_PARTS - 1 and w < len(wanted):
+                    pair_dot(w, place + ring - 1 - t, place + 1 + t, t == 0)
                 if flow == ordered[3] and ended < bits - 1:
                     end_tally(ended)
                     ended += 1
@@ -364,15 +387,20 @@
                 jnp.sqrt(jnp.sum(norm_sums[0, w] + norm_sums[1, w], keepdims=True))
                 for w in range(GROUP)
             ]
-        else:
-            q_pair.wait_recv()
-            loads[5].wait()
-        source = ks if step == 0 else qs
-        for w in range(2):
+
+        def last_dot(w):
             for h in range(LANE_PARTS):
                 take_block(2 * w + h, turn)
-            act_dot(1, w, source, own)
-            act_dot(1, w, source, other)
+            if w >= len(wanted):
+                return
+            if in_pairs:
+                pair_dot(w, place, place + ring // 2, False)
+            else:
+                act_dot(1, w, wanted[w], own)
+                act_dot(1, w, wanted[w], other)
+
+        last_dot(0)
+        last_dot(1)
         while ended < bits:
             end_tally(ended)
             ended += 1
@@ -384,10 +412,7 @@
         if step == 0:
             hid_gates(scales, whole)
             grad(2)
-            for h in range(LANE_PARTS):
-                take_block(4 + h, turn)
-            act_dot(1, 2, us, own)
-            act_dot(1, 2, us, other)
+            last_dot(2)
         ring_sent(1)
         for copy in tallies:
             copy.wait_send()
@@ -402,7 +427,7 @@
     hid_copies = []
 
     def send_hid(slot, source, target, device):
-        copy = remote(source, target, hid_send, hid_recv.at[slot], device)
+        copy = remote(source, target, hid_send.at[slot // 2], hid_recv.at[slot], device)
         copy.start()
         return copy
 
@@ -422,12 +447,16 @@
 
     for side in range(CORES):
         hidden_of(side, 0, tokens)
-    for h in range(LANE_PARTS):
-        take_block(4 + h, turn)
+    last_dot(2)
     near_copy = send_hid(2 * len(TILES), hq.at[other, :], near_hid, sibling)
     send_tile(0)
     wide = ((1,), (1,))
     stripe = half // STRIPES
+
+    def tile_sent(t):
+        first, last = tiles[t]
+        both = far_hid.at[:, first:last, :]
+        remote(both, both, hid_send.at[t], hid_recv.at[2 * t], across).wait_send()
 
     def near_stripes(first, last):
         def one(c, carry):
@@ -445,8 +474,8 @@
     near[...] = ((mine + theirs) * scales[2]).astype(BF16)
     w_copy.wait()
     near_stripes(0, 2)
-    for t in range(1, len(TILES)):
-        send_tile(t)
+    send_tile(1)
+    send_tile(2)
     far_w2_copy = remote(far_w2.at[0:2], far_w2.at[0:2], w2_send, w2_recv, across)
     far_w2_copy.wait_recv()
     far_pair = pair(5, far_w2.at[0:2], far_w2.at[2:4])
@@ -477,12 +506,13 @@
 
         lax.fori_loop(0, STRIPES, far_cols_of, 0)
     pltpu.make_async_copy(staged, out, out_sem).wait()
-    hid_sent = us.at[: (CORES + 1) * tokens * cols // rows, :]
+    for t in range(len(TILES)):
+        tile_sent(t)
+    near_copy.wait_send()
     near_w2_copy.wait_send()
     far_w2_copy.wait_send()
     far_pair.wait_send()
     w_share.wait_send()
-    remote(hid_sent, hid_sent, hid_send, hid_recv.at[0], sibling).wait_send()
     for copy in (k_pair, u_pair, q_pair):
         copy.wait_send()
 
@@ -562,7 +592,7 @@
             dma,
             dma,
             dma,
-            dma,
+            dma((len(TILES) + 1,)),
             dma((2 * len(TILES) + 1,)),
             dma((7,)),
             dma,

time: 99 us -> 98.7 us (level)
  no operation moved by 1% of the time
where the time goes in v5:
time: 98.7 us; the launch traced here: 97.9 us
  Pallas kernels  97.9 us (99%)
    pallas_call x1, Pallas kernels, shards(): pl.pallas_call(functools.partial(layer_kernel, n_ctx), out_shape=jax.Shap...  95.3 us
    pallas_call x1, Pallas kernels, shards(): pl.pallas_call(copy_kernel, out_shape=jax.ShapeDtypeStruct((tokens, half)...  2.53 us

profile of v5, /device:TPU:0, one launch (start us, length us, event | category | flops | bytes accessed | tf_op | source)
XLA Modules:
  0.0 97.9 jit_solution(18102629123677948610)
XLA Ops:
  0.0 95.3 %shard_map.82.source = bf16[512,2560]{1,0:T(8,128)(2,1)} custom-call(bf16[512,1024]{1,0:T(8,128)(2,1)} %q.1, bf16[512,1024]{1,0:T(8,128)(2,1)} %k.1, bf16[512,1024]{1,0:T(8,128)(2,1)} %v.1, f32[1,512]{1,0:T(1,128)} %bitcast.7, bf16[1024,512]{1,0:T(8,128)(2,1)} %bitcast.4, bf16[1024,512]{1,0:T(8,128)(2,1)} %bitcast.5, bf16[512,1024]{1,0:T(8,128)(2,1)} %bitcast.6, ...), custom_call_target="tpu_custom_call" | custom-call | tf_op jit(solution)/shard_map/pallas_call | solution.py:546
  95.3 2.5 %shard_map.83 = bf16[512,2560]{1,0:T(8,128)(2,1)} custom-call(bf16[512,2560]{1,0:T(8,128)(2,1)} %shard_map.82.source), custom_call_target="tpu_custom_call" | custom-call | tf_op jit(solution)/shard_map/pallas_call | solution.py:604

commit v6 on v5

--- a/solution.py
+++ b/solution.py
@@ -15,7 +15,7 @@
 LANE_PARTS = 2
 CORES = 2
 RING_ROWS = 4
-TILES = (4, 2, 2)
+TILES = (1, 1)
 PIECES = 2
 STRIPES = 5
 COPY_PIECES = 8
@@ -55,7 +55,7 @@
         hq, near_hid, far_hid, near_w2, far_w2, far_scale, scale_out,
         w_near, w_far, near, total_out, staged,
         ring_send, ring_recv, pair_send, pair_recv, tally_send, tally_recv,
-        side_send, side_recv, w2_send, w2_recv, near_send, near_recv, hid_send, hid_recv, local_sem, out_sem,
+        side_send, side_recv, w2_send, w2_recv, relay_sem, near_send, near_recv, hid_send, hid_recv, local_sem, out_sem,
     ) = scratch
     tokens, rows = k.shape
     cols = first0.shape[1]
@@ -250,10 +250,14 @@
             grads[flow, at, :] = total.astype(BF16)
             send_sum(flow, to_right, s + 1)
 
-        def send_w2(flow, number):
-            here = chunk(number)
-            target = far_w2.at[flow % LANE_PARTS, here, :]
-            remote(blocks.at[flow, here, :], target, w2_send, w2_recv, across).start()
+        def send_w2(flow, offset):
+            here = chunk(place + ring + offset)
+            if abs(offset) < ring // 2:
+                slot = 1 if offset == ring // 2 - 1 else 0
+                target = far_w2.at[flow % LANE_PARTS, here, :]
+                remote(
+                    blocks.at[flow, here, :], target, w2_send, w2_recv.at[slot], across
+                ).start()
             target = near_w2.at[flow % LANE_PARTS, here, :]
             remote(
                 blocks.at[flow, here, :], target, near_send, near_recv, sibling
@@ -315,7 +319,7 @@
             send_block(flow, True, 0)
             send_block(flow, False, 0)
             if step == STEPS - 1 and w == 2:
-                send_w2(flow, place)
+                send_w2(flow, 0)
             part = square_sum(rounded.astype(F32))
             tally[0, w] = part if h == 0 else tally[0, w] + part
         tallies = []
@@ -344,7 +348,7 @@
                 if t < count - 1:
                     send_block(flow, to_right, t + 1)
                 if step == STEPS - 1 and flow // LANE_PARTS == 2:
-                    send_w2(flow, place + (ring - 1 - t if to_right else 1 + t))
+                    send_w2(flow, -1 - t if to_right else 1 + t)
 
         if step > 0:
             q_pair.wait_recv()
@@ -472,15 +476,20 @@
     mine = dot(hq[own, :], jnp.concatenate([blocks[4], blocks[5]], axis=1), wide)
     theirs = dot(near_hid[...], jnp.concatenate([near_w2[0], near_w2[1]], axis=1), wide)
     near[...] = ((mine + theirs) * scales[2]).astype(BF16)
+    for t in range(1, len(TILES)):
+        send_tile(t)
     w_copy.wait()
     near_stripes(0, 2)
-    send_tile(1)
-    send_tile(2)
-    far_w2_copy = remote(far_w2.at[0:2], far_w2.at[0:2], w2_send, w2_recv, across)
-    far_w2_copy.wait_recv()
+    next_w2 = far_w2.at[0:2, chunk(place + ring // 2 - 1), :]
+    remote(next_w2, next_w2, w2_send, w2_recv.at[1], across).wait_recv()
+    relay = remote(next_w2, next_w2, relay_sem.at[0], relay_sem.at[1], left)
+    relay.start()
+    near_stripes(2, STRIPES)
+    most_w2 = far_w2.at[0:2, : (ring - 2) * size, :]
+    remote(most_w2, most_w2, w2_send, w2_recv.at[0], across).wait_recv()
+    relay.wait_recv()
     far_pair = pair(5, far_w2.at[0:2], far_w2.at[2:4])
     far_pair.start()
-    near_stripes(2, STRIPES)
     scale_swap.wait()
     w_share.wait_recv()
     far_pair.wait_recv()
@@ -510,7 +519,9 @@
         tile_sent(t)
     near_copy.wait_send()
     near_w2_copy.wait_send()
-    far_w2_copy.wait_send()
+    sent_w2 = far_w2.at[0:2, : (ring - 1) * size, :]
+    remote(sent_w2, sent_w2, w2_send, w2_recv.at[0], across).wait_send()
+    relay.wait_send()
     far_pair.wait_send()
     w_share.wait_send()
     for copy in (k_pair, u_pair, q_pair):
@@ -589,7 +600,8 @@
             dma((2,)),
             dma((2,)),
             dma,
-            dma,
+            dma((2,)),
+            dma((2,)),
             dma,
             dma,
             dma((len(TILES) + 1,)),

time: 98.7 us -> 97.1 us (0.984)
  Pallas kernels: 97.9 us -> 96.2 us
    pallas_call x1, Pallas kernels: 95.3 us -> 93.7 us  [shards(): pl.pallas_call(functools.partial(layer_kernel, n_ctx), out_shape=jax.Shap...]
where the time goes in v6:
time: 97.1 us; the launch traced here: 96.2 us
  Pallas kernels  96.2 us (99%)
    pallas_call x1, Pallas kernels, shards(): pl.pallas_call(functools.partial(layer_kernel, n_ctx), out_shape=jax.Shap...  93.7 us
    pallas_call x1, Pallas kernels, shards(): pl.pallas_call(copy_kernel, out_shape=jax.ShapeDtypeStruct((tokens, half)...  2.53 us

profile of v6, /device:TPU:0, one launch (start us, length us, event | category | flops | bytes accessed | tf_op | source)
XLA Modules:
  0.0 96.2 jit_solution(14697491997361875893)
XLA Ops:
  0.0 93.7 %shard_map.82.source = bf16[512,2560]{1,0:T(8,128)(2,1)} custom-call(bf16[512,1024]{1,0:T(8,128)(2,1)} %q.1, bf16[512,1024]{1,0:T(8,128)(2,1)} %k.1, bf16[512,1024]{1,0:T(8,128)(2,1)} %v.1, f32[1,512]{1,0:T(1,128)} %bitcast.7, bf16[1024,512]{1,0:T(8,128)(2,1)} %bitcast.4, bf16[1024,512]{1,0:T(8,128)(2,1)} %bitcast.5, bf16[512,1024]{1,0:T(8,128)(2,1)} %bitcast.6, ...), custom_call_target="tpu_custom_call" | custom-call | tf_op jit(solution)/shard_map/pallas_call | solution.py:557
  93.7 2.5 %shard_map.83 = bf16[512,2560]{1,0:T(8,128)(2,1)} custom-call(bf16[512,2560]{1,0:T(8,128)(2,1)} %shard_map.82.source), custom_call_target="tpu_custom_call" | custom-call | tf_op jit(solution)/shard_map/pallas_call | solution.py:616

commit v7 on v6

--- a/solution.py
+++ b/solution.py
@@ -18,7 +18,6 @@
 TILES = (1, 1)
 PIECES = 2
 STRIPES = 5
-COPY_PIECES = 8
 
 
 def ring_place(chip, width):
@@ -53,9 +52,9 @@
         ks, us, qs, vin, kt, ut, first0, first1, in2, first2,
         acts, mid, grads, blocks, arrived, kept, tally, tally_in, norm_sums,
         hq, near_hid, far_hid, near_w2, far_w2, far_scale, scale_out,
-        w_near, w_far, near, total_out, staged,
+        w_near, w_far, near, total_out,
         ring_send, ring_recv, pair_send, pair_recv, tally_send, tally_recv,
-        side_send, side_recv, w2_send, w2_recv, relay_sem, near_send, near_recv, hid_send, hid_recv, local_sem, out_sem,
+        side_send, side_recv, w2_send, w2_recv, relay_sem, near_send, near_recv, hid_send, hid_recv, local_sem,
     ) = scratch
     tokens, rows = k.shape
     cols = first0.shape[1]
@@ -509,12 +508,10 @@
         def far_cols_of(c, carry):
             lanes = pl.ds(pl.multiple_of(c * stripe, 128), stripe)
             added = total_out[at, lanes] + dot(near[at, :], w_far[:, lanes])
-            staged[at, lanes] = added.astype(BF16)
-            pltpu.make_async_copy(staged.at[at, lanes], out.at[at, lanes], out_sem).start()
+            out[at, lanes] = added.astype(BF16)
             return carry
 
         lax.fori_loop(0, STRIPES, far_cols_of, 0)
-    pltpu.make_async_copy(staged, out, out_sem).wait()
     for t in range(len(TILES)):
         tile_sent(t)
     near_copy.wait_send()
@@ -528,21 +525,6 @@
         copy.wait_send()
 
 
-def copy_kernel(source, target, held, in_sem, out_sem):
-    rows = held.shape[0] // COPY_PIECES
-    pieces = [pl.ds(piece * rows, rows) for piece in range(COPY_PIECES)]
-    reads = [
-        pltpu.make_async_copy(source.at[at, :], held.at[at, :], in_sem.at[piece])
-        for piece, at in enumerate(pieces)
-    ]
-    for read in reads:
-        read.start()
-    for read, at in zip(reads, pieces):
-        read.wait()
-        pltpu.make_async_copy(held.at[at, :], target.at[at, :], out_sem).start()
-    pltpu.make_async_copy(held, target, out_sem).wait()
-
-
 def shards(n_ctx, queries, keys, values, rates, w_up, w_gate, w_down, w_out):
     tokens, rows = keys.shape
     cols = w_up.shape[2] // CORES
@@ -554,11 +536,11 @@
     vmem = pl.BlockSpec(memory_space=pltpu.VMEM)
     anywhere = pl.BlockSpec(memory_space=pl.ANY)
     dma = pltpu.SemaphoreType.DMA
-    mixed = pl.pallas_call(
+    return pl.pallas_call(
         functools.partial(layer_kernel, n_ctx),
-        out_shape=jax.ShapeDtypeStruct((tokens, half), BF16),
+        out_shape=pltpu.VMEM((tokens, half), BF16),
         in_specs=[anywhere] * 3 + [vmem] + [anywhere] * 4,
-        out_specs=anywhere,
+        out_specs=vmem,
         scratch_shapes=[
             pltpu.VMEM((2 * tokens, rows), BF16),
             pltpu.VMEM((2 * tokens, rows), BF16),
@@ -590,7 +572,6 @@
             pltpu.VMEM((rows, half), BF16),
             pltpu.VMEM((tokens, rows), BF16),
             pltpu.VMEM((tokens, half), F32),
-            pltpu.VMEM((tokens, half), BF16),
             dma((2,)),
             dma((flows, 2 * (ring - 1))),
             dma((6,)),
@@ -607,19 +588,11 @@
             dma((len(TILES) + 1,)),
             dma((2 * len(TILES) + 1,)),
             dma((7,)),
-            dma,
         ],
         compiler_params=pltpu.CompilerParams(
             collective_id=0, has_side_effects=True, vmem_limit_bytes=60 << 20
         ),
     )(queries, keys, values, rates.T, w_up[0], w_gate[0], w_down[0], w_out)
-    return pl.pallas_call(
-        copy_kernel,
-        out_shape=jax.ShapeDtypeStruct((tokens, half), BF16),
-        in_specs=[anywhere],
-        out_specs=anywhere,
-        scratch_shapes=[pltpu.VMEM((tokens, half), BF16), dma((COPY_PIECES,)), dma],
-    )(mixed)
 
 
 def solution(mesh):

time: 97.1 us -> 95.3 us (0.981)
  Pallas kernels: 96.2 us -> 92.9 us
  local copies, waits for them, and re-layouts: 0 us -> 1.49 us
    pallas_call x2 -> x1, Pallas kernels: 96.2 us -> 92.9 us  [shards(): pl.pallas_call(functools.partial(layer_kernel, n_ctx), out_shape=pltpu.VM...]
    unnamed x0 -> x1, local copies, waits for them, and re-layouts: none -> 1.49 us
where the time goes in v7:
time: 95.3 us; the launch traced here: 94.4 us
  Pallas kernels  92.9 us (97%)
  local copies, waits for them, and re-layouts  1.49 us (2%)
    pallas_call x1, Pallas kernels, shards(): pl.pallas_call(functools.partial(layer_kernel, n_ctx), out_shape=pltpu.VM...  92.9 us

profile of v7, /device:TPU:0, one launch (start us, length us, event | category | flops | bytes accessed | tf_op | source)
XLA Modules:
  0.0 94.4 jit_solution(13125297968141296908)
XLA Ops:
  0.0 92.9 %shard_map.82 = bf16[512,2560]{1,0:T(8,128)(2,1)S(1)} custom-call(bf16[512,1024]{1,0:T(8,128)(2,1)} %q.1, bf16[512,1024]{1,0:T(8,128)(2,1)} %k.1, bf16[512,1024]{1,0:T(8,128)(2,1)} %v.1, f32[1,512]{1,0:T(1,128)} %bitcast.7, bf16[1024,512]{1,0:T(8,128)(2,1)} %bitcast.4, bf16[1024,512]{1,0:T(8,128)(2,1)} %bitcast.5, bf16[512,1024]{1,0:T(8,128)(2,1)} %bitcast.6, ...), custom_call_target="tpu_custom_call" | custom-call | tf_op jit(solution)/shard_map/pallas_call | solution.py:539
  92.9 1.5 %copy.10 = bf16[512,2560]{1,0:T(8,128)(2,1)} copy(bf16[512,2560]{1,0:T(8,128)(2,1)S(1)} %shard_map.82) | data formatting | bytes 5242880

commit v8 on v7

--- a/solution.py
+++ b/solution.py
@@ -104,7 +104,7 @@
     for load in loads[:5]:
         load.start()
 
-    partners = [right, left, sibling, across, diagonal] + tally_partners
+    partners = [right, left, sibling, across, diagonal]
     barrier = pltpu.get_barrier_semaphore()
     for target in partners:
         pl.semaphore_signal(barrier, inc=1, device_id=target, device_id_type=MESH)

time: 95.3 us -> 94.9 us (level)
  no operation moved by 1% of the time
where the time goes in v8:
time: 94.9 us; the launch traced here: 94.5 us
  Pallas kernels  93 us (98%)
  local copies, waits for them, and re-layouts  1.49 us (2%)
    pallas_call x1, Pallas kernels, shards(): pl.pallas_call(functools.partial(layer_kernel, n_ctx), out_shape=pltpu.VM...  93 us

profile of v8, /device:TPU:0, one launch (start us, length us, event | category | flops | bytes accessed | tf_op | source)
XLA Modules:
  0.0 94.5 jit_solution(12805114624214052294)
XLA Ops:
  0.0 93.0 %shard_map.82 = bf16[512,2560]{1,0:T(8,128)(2,1)S(1)} custom-call(bf16[512,1024]{1,0:T(8,128)(2,1)} %q.1, bf16[512,1024]{1,0:T(8,128)(2,1)} %k.1, bf16[512,1024]{1,0:T(8,128)(2,1)} %v.1, f32[1,512]{1,0:T(1,128)} %bitcast.7, bf16[1024,512]{1,0:T(8,128)(2,1)} %bitcast.4, bf16[1024,512]{1,0:T(8,128)(2,1)} %bitcast.5, bf16[512,1024]{1,0:T(8,128)(2,1)} %bitcast.6, ...), custom_call_target="tpu_custom_call" | custom-call | tf_op jit(solution)/shard_map/pallas_call | solution.py:539
  93.0 1.5 %copy.10 = bf16[512,2560]{1,0:T(8,128)(2,1)} copy(bf16[512,2560]{1,0:T(8,128)(2,1)S(1)} %shard_map.82) | data formatting | bytes 5242880

commit v9 on v8

--- a/solution.py
+++ b/solution.py
@@ -17,7 +17,7 @@
 RING_ROWS = 4
 TILES = (1, 1)
 PIECES = 2
-STRIPES = 5
+STRIPES = 2
 
 
 def ring_place(chip, width):
@@ -478,12 +478,12 @@
     for t in range(1, len(TILES)):
         send_tile(t)
     w_copy.wait()
-    near_stripes(0, 2)
+    near_stripes(0, 1)
     next_w2 = far_w2.at[0:2, chunk(place + ring // 2 - 1), :]
     remote(next_w2, next_w2, w2_send, w2_recv.at[1], across).wait_recv()
     relay = remote(next_w2, next_w2, relay_sem.at[0], relay_sem.at[1], left)
     relay.start()
-    near_stripes(2, STRIPES)
+    near_stripes(1, STRIPES)
     most_w2 = far_w2.at[0:2, : (ring - 2) * size, :]
     remote(most_w2, most_w2, w2_send, w2_recv.at[0], across).wait_recv()
     relay.wait_recv()

time: 94.9 us -> 94.7 us (level)
  no operation moved by 1% of the time
where the time goes in v9:
time: 94.7 us; the launch traced here: 93.9 us
  Pallas kernels  92.4 us (98%)
  local copies, waits for them, and re-layouts  1.49 us (2%)
    pallas_call x1, Pallas kernels, shards(): pl.pallas_call(functools.partial(layer_kernel, n_ctx), out_shape=pltpu.VM...  92.4 us

profile of v9, /device:TPU:0, one launch (start us, length us, event | category | flops | bytes accessed | tf_op | source)
XLA Modules:
  0.0 93.9 jit_solution(16414206616047959612)
XLA Ops:
  0.0 92.4 %shard_map.82 = bf16[512,2560]{1,0:T(8,128)(2,1)S(1)} custom-call(bf16[512,1024]{1,0:T(8,128)(2,1)} %q.1, bf16[512,1024]{1,0:T(8,128)(2,1)} %k.1, bf16[512,1024]{1,0:T(8,128)(2,1)} %v.1, f32[1,512]{1,0:T(1,128)} %bitcast.7, bf16[1024,512]{1,0:T(8,128)(2,1)} %bitcast.4, bf16[1024,512]{1,0:T(8,128)(2,1)} %bitcast.5, bf16[512,1024]{1,0:T(8,128)(2,1)} %bitcast.6, ...), custom_call_target="tpu_custom_call" | custom-call | tf_op jit(solution)/shard_map/pallas_call | solution.py:539
  92.4 1.5 %copy.10 = bf16[512,2560]{1,0:T(8,128)(2,1)} copy(bf16[512,2560]{1,0:T(8,128)(2,1)S(1)} %shard_map.82) | data formatting | bytes 5242880
